TPU v7x, 32 devices: a whole 2x2x4 slice. The times are simulated.
32 devices in a mesh: dp: 8 (over z, x), tensor: 4 (over y, core).
Axes of the slice: x: 2, y: 2, z: 4, core: 2. Of those that a mesh axis runs over, the one named last changes fastest.
Arguments:
- frames: bfloat16 [12288, 768], P(('dp', 'tensor')), may hold values from -6 to 6
- segments: int32 [8, 1536], P('dp'), may hold values from 0 to 15, never falling along the last dimension, each value on 1 to 768 neighbouring positions
- norm1_gain: float32 [768], P(('dp', 'tensor')), may hold values from 0.25 to 1.75
- norm1_shift: float32 [768], P(('dp', 'tensor')), may hold values from -1.5 to 1.5
- in_weight: bfloat16 [768, 3, 768], P('dp', None, 'tensor'), may hold values from -0.21875 to 0.21875
- proj_bias: bfloat16 [2, 12, 64], P(None, 'tensor', 'dp'), may hold values from -1.5 to 1.5
- out_weight: bfloat16 [768, 768], P('tensor', 'dp'), may hold values from -0.875 to 0.875
- out_bias: float32 [768], P(('dp', 'tensor')), may hold values from -1.5 to 1.5
- norm2_gain: float32 [768], P(('dp', 'tensor')), may hold values from 0.25 to 1.75
- norm2_shift: float32 [768], P(('dp', 'tensor')), may hold values from -1.5 to 1.5
- fc1_weight: bfloat16 [768, 3072], P('dp', 'tensor'), may hold values from -0.21875 to 0.21875
- fc1_bias: bfloat16 [48, 64], P('tensor', 'dp'), may hold values from -1.5 to 1.5
- fc2_weight: bfloat16 [3072, 768], P('tensor', 'dp'), may hold values from -0.109375 to 0.109375
- fc2_bias: float32 [768], P(('dp', 'tensor')), may hold values from -1.5 to 1.5
- cotangent: bfloat16 [12288, 768], P(('dp', 'tensor')), may hold values from -6 to 6
Outputs:
- output: bfloat16 [12288, 768], P(('dp', 'tensor'))
- grad_frames: float32 [12288, 768], P(('dp', 'tensor'))
- grad_norm1_gain: float32 [768], P(('dp', 'tensor'))
- grad_norm1_shift: float32 [768], P(('dp', 'tensor'))
- grad_in_weight: float32 [768, 3, 768], P('dp', None, 'tensor')
- grad_proj_bias: float32 [2, 12, 64], P(None, 'tensor', 'dp')
- grad_out_weight: float32 [768, 768], P('tensor', 'dp')
- grad_out_bias: float32 [768], P(('dp', 'tensor'))
- grad_norm2_gain: float32 [768], P(('dp', 'tensor'))
- grad_norm2_shift: float32 [768], P(('dp', 'tensor'))
- grad_fc1_weight: float32 [768, 3072], P('dp', 'tensor')
- grad_fc1_bias: float32 [48, 64], P('tensor', 'dp')
- grad_fc2_weight: float32 [3072, 768], P('tensor', 'dp')
- grad_fc2_bias: float32 [768], P(('dp', 'tensor'))
Inputs may be any that keep to these rules, and one draw needn't show every extreme that they name: `segments`: within each sequence the numbers never fall, every number appears, each covers 1 to 768 frames, and one covers exactly 768.
All inputs are finite; a program needn't handle non-finite values.
Results may differ from a plain program's by a relative error of at most 0.015.
Values may be sent and summed in bfloat16 or wider, within the bound.
A program may use at most 128 MiB of HBM per device.

v0:
```python
import jax
import jax.numpy as jnp
from jax import lax
from jax.sharding import PartitionSpec as P

HD = 64


def layer_norm(row_block, norm_gain, norm_shift):
    row_mean = jnp.mean(row_block, axis=-1, keepdims=True)
    centred = row_block - row_mean
    row_var = jnp.mean(centred * centred, axis=-1, keepdims=True)
    return centred * lax.rsqrt(row_var + 1e-05) * norm_gain + norm_shift


def gelu_exact(values_in):
    return jax.nn.gelu(values_in, approximate=False)


def contract(pattern, left, right):
    return jnp.einsum(pattern, left, right, preferred_element_type=jnp.float32)


def on_device(
    frames,
    segments,
    norm1_gain,
    norm1_shift,
    in_weight,
    proj_bias,
    out_weight,
    out_bias,
    norm2_gain,
    norm2_shift,
    fc1_weight,
    fc1_bias,
    fc2_weight,
    fc2_bias,
    cotangent,
):
    gain_one, shift_one, gain_two, shift_two, bias_out, bias_fc2 = (
        lax.all_gather(norm1_gain, ("dp", "tensor"), axis=0, tiled=True),
        lax.all_gather(norm1_shift, ("dp", "tensor"), axis=0, tiled=True),
        lax.all_gather(norm2_gain, ("dp", "tensor"), axis=0, tiled=True),
        lax.all_gather(norm2_shift, ("dp", "tensor"), axis=0, tiled=True),
        lax.all_gather(out_bias, ("dp", "tensor"), axis=0, tiled=True),
        lax.all_gather(fc2_bias, ("dp", "tensor"), axis=0, tiled=True),
    )
    in_full, proj_full, out_full, fc1_full, fc1b_full, fc2_full = (
        lax.all_gather(in_weight, "dp", axis=0, tiled=True),
        lax.all_gather(proj_bias, "dp", axis=2, tiled=True),
        lax.all_gather(out_weight, "dp", axis=1, tiled=True),
        lax.all_gather(fc1_weight, "dp", axis=0, tiled=True),
        lax.all_gather(fc1_bias, "dp", axis=1, tiled=True),
        lax.all_gather(fc2_weight, "dp", axis=1, tiled=True),
    )
    model_width = frames.shape[1]
    doc_ids = segments[0]
    seq_length = doc_ids.shape[0]
    heads_width = in_full.shape[2]
    local_heads = heads_width // HD
    block_rows = min(512, seq_length)
    num_blocks = seq_length // block_rows
    rows_in = frames.astype(jnp.float32)
    normed = layer_norm(rows_in, gain_one, shift_one).astype(jnp.bfloat16)
    normed_all = lax.all_gather(normed, "tensor", axis=0, tiled=True)
    projected = jnp.dot(
        normed_all,
        in_full.reshape(model_width, 3 * heads_width),
        preferred_element_type=jnp.float32,
    ).reshape(seq_length, 3, heads_width)
    bias_pair = proj_full.astype(jnp.float32).reshape(2, heads_width)
    query = (
        (projected[:, 0] + bias_pair[0]).astype(jnp.bfloat16).reshape(seq_length, local_heads, HD)
    )
    keys_all = projected[:, 1].astype(jnp.bfloat16).reshape(seq_length, local_heads, HD)
    values_all = (
        (projected[:, 2] + bias_pair[1]).astype(jnp.bfloat16).reshape(seq_length, local_heads, HD)
    )

    def scores_of(query_block, doc_block):
        raw_scores = contract("qhe,khe->hqk", query_block, keys_all) * 0.125
        same_doc = doc_block[:, None] == doc_ids[None, :]
        return jnp.where(same_doc[None], raw_scores, -1e30)

    def forward_block(block_index):
        block_start = block_index * block_rows
        query_block = lax.dynamic_slice_in_dim(query, block_start, block_rows, 0)
        doc_block = lax.dynamic_slice_in_dim(doc_ids, block_start, block_rows, 0)
        scores = scores_of(query_block, doc_block)
        row_max = jnp.max(scores, axis=-1, keepdims=True)
        exp_scores = jnp.exp(scores - row_max)
        row_total = jnp.sum(exp_scores, axis=-1, keepdims=True)
        attn_probs = (exp_scores / row_total).astype(jnp.bfloat16)
        block_mixed = contract("hqk,khe->qhe", attn_probs, values_all)
        log_total = (row_max + jnp.log(row_total))[..., 0]
        return (block_mixed.astype(jnp.bfloat16).reshape(block_rows, heads_width), log_total)

    mixed_blocks, log_totals = lax.map(forward_block, jnp.arange(num_blocks, dtype=jnp.int32))
    attn_mixed = mixed_blocks.reshape(seq_length, heads_width)
    attn_partial = jnp.dot(attn_mixed, out_full, preferred_element_type=jnp.float32)
    attended = lax.psum_scatter(attn_partial, "tensor", scatter_dimension=0, tiled=True) + bias_out
    middle = rows_in + attended
    normed_two = layer_norm(middle, gain_two, shift_two).astype(jnp.bfloat16)
    grad_out = cotangent.astype(jnp.float32)
    normed_two_all = lax.all_gather(normed_two, "tensor", axis=0, tiled=True)
    hidden = jnp.dot(
        normed_two_all, fc1_full, preferred_element_type=jnp.float32
    ) + fc1b_full.astype(jnp.float32).reshape(-1)
    active = gelu_exact(hidden).astype(jnp.bfloat16)
    branch = (
        lax.psum_scatter(
            jnp.dot(active, fc2_full, preferred_element_type=jnp.float32).astype(jnp.bfloat16),
            "tensor",
            scatter_dimension=0,
            tiled=True,
        ).astype(jnp.float32)
        + bias_fc2
    )
    output = (middle + branch).astype(jnp.bfloat16)
    grad_branch_all = lax.all_gather(cotangent, "tensor", axis=0, tiled=True)
    grad_fc2 = contract("lf,ld->fd", active, grad_branch_all)
    grad_active = contract("ld,fd->lf", grad_branch_all, fc2_full)
    grad_hidden = jax.vjp(gelu_exact, hidden)[1](grad_active)[0].astype(jnp.bfloat16)
    grad_fc1 = contract("ld,lf->df", normed_two_all, grad_hidden)
    grad_fc1b = jnp.sum(grad_hidden.astype(jnp.float32), axis=0).reshape(fc1b_full.shape)
    grad_normed_two = lax.psum_scatter(
        contract("lf,df->ld", grad_hidden, fc1_full).astype(jnp.bfloat16),
        "tensor",
        scatter_dimension=0,
        tiled=True,
    ).astype(jnp.float32)
    grad_bias_fc2 = jnp.sum(grad_out, axis=0)
    norm_back_two = jax.vjp(layer_norm, middle, gain_two, shift_two)[1]
    grad_mid_norm, grad_gain_two, grad_shift_two = norm_back_two(grad_normed_two)
    grad_middle = grad_out + grad_mid_norm
    grad_attended = grad_middle.astype(jnp.bfloat16)
    grad_bias_out = jnp.sum(grad_attended.astype(jnp.float32), axis=0)
    grad_att_all = lax.all_gather(grad_attended, "tensor", axis=0, tiled=True)
    grad_out_w = contract("lh,ld->hd", attn_mixed, grad_att_all)
    grad_mixed = (
        contract("ld,hd->lh", grad_att_all, out_full)
        .astype(jnp.bfloat16)
        .reshape(seq_length, local_heads, HD)
    )

    def backward_block(carried, block_index):
        grad_keys_acc, grad_values_acc = carried
        block_start = block_index * block_rows
        query_block = lax.dynamic_slice_in_dim(query, block_start, block_rows, 0)
        doc_block = lax.dynamic_slice_in_dim(doc_ids, block_start, block_rows, 0)
        grad_block = lax.dynamic_slice_in_dim(grad_mixed, block_start, block_rows, 0)
        scores = scores_of(query_block, doc_block)
        attn_probs = jnp.exp(scores - log_totals[block_index][..., None])
        grad_probs = contract("qhe,khe->hqk", grad_block, values_all)
        row_inner = jnp.sum(attn_probs * grad_probs, axis=-1, keepdims=True)
        grad_scores = (attn_probs * (grad_probs - row_inner)).astype(jnp.bfloat16)
        grad_query_block = contract("hqk,khe->qhe", grad_scores, keys_all) * 0.125
        grad_keys_acc = grad_keys_acc + contract("hqk,qhe->khe", grad_scores, query_block) * 0.125
        grad_values_acc = grad_values_acc + contract(
            "hqk,qhe->khe", attn_probs.astype(jnp.bfloat16), grad_block
        )
        return ((grad_keys_acc, grad_values_acc), grad_query_block)

    empty_acc = jnp.zeros((seq_length, local_heads, HD), jnp.float32)
    (grad_keys_all, grad_values_all), grad_query_blocks = lax.scan(
        backward_block, (empty_acc, empty_acc), jnp.arange(num_blocks, dtype=jnp.int32)
    )
    grad_proj = jnp.stack(
        [
            grad_query_blocks.reshape(seq_length, heads_width),
            grad_keys_all.reshape(seq_length, heads_width),
            grad_values_all.reshape(seq_length, heads_width),
        ],
        axis=1,
    ).astype(jnp.bfloat16)
    grad_proj_sums = jnp.sum(grad_proj.astype(jnp.float32), axis=0)
    grad_proj_b = jnp.stack([grad_proj_sums[0], grad_proj_sums[2]], axis=0).reshape(
        2, local_heads, HD
    )
    grad_in_w = contract("ld,lcf->dcf", normed_all, grad_proj)
    grad_normed = lax.psum_scatter(
        contract("lcf,dcf->ld", grad_proj, in_full).astype(jnp.bfloat16),
        "tensor",
        scatter_dimension=0,
        tiled=True,
    ).astype(jnp.float32)
    norm_back_one = jax.vjp(layer_norm, rows_in, gain_one, shift_one)[1]
    grad_rows_norm, grad_gain_one, grad_shift_one = norm_back_one(grad_normed)
    grad_frames = grad_middle + grad_rows_norm
    g_in, g_proj, g_out, g_fc1, g_fc1b, g_fc2 = (
        lax.psum_scatter(grad_in_w, "dp", scatter_dimension=0, tiled=True),
        lax.psum_scatter(grad_proj_b, "dp", scatter_dimension=2, tiled=True),
        lax.psum_scatter(grad_out_w, "dp", scatter_dimension=1, tiled=True),
        lax.psum_scatter(grad_fc1, "dp", scatter_dimension=0, tiled=True),
        lax.psum_scatter(grad_fc1b, "dp", scatter_dimension=1, tiled=True),
        lax.psum_scatter(grad_fc2, "dp", scatter_dimension=1, tiled=True),
    )
    v_gain_one, v_shift_one, v_gain_two, v_shift_two, v_bias_out, v_bias_fc2 = (
        lax.psum_scatter(grad_gain_one, ("dp", "tensor"), scatter_dimension=0, tiled=True),
        lax.psum_scatter(grad_shift_one, ("dp", "tensor"), scatter_dimension=0, tiled=True),
        lax.psum_scatter(grad_gain_two, ("dp", "tensor"), scatter_dimension=0, tiled=True),
        lax.psum_scatter(grad_shift_two, ("dp", "tensor"), scatter_dimension=0, tiled=True),
        lax.psum_scatter(grad_bias_out, ("dp", "tensor"), scatter_dimension=0, tiled=True),
        lax.psum_scatter(grad_bias_fc2, ("dp", "tensor"), scatter_dimension=0, tiled=True),
    )
    return (
        output,
        grad_frames,
        v_gain_one,
        v_shift_one,
        g_in,
        g_proj,
        g_out,
        v_bias_out,
        v_gain_two,
        v_shift_two,
        g_fc1,
        g_fc1b,
        g_fc2,
        v_bias_fc2,
    )


def solution(mesh):
    in_specs = (
        P(("dp", "tensor"), None),
        P("dp", None),
        P(("dp", "tensor")),
        P(("dp", "tensor")),
        P("dp", None, "tensor"),
        P(None, "tensor", "dp"),
        P("tensor", "dp"),
        P(("dp", "tensor")),
        P(("dp", "tensor")),
        P(("dp", "tensor")),
        P("dp", "tensor"),
        P("tensor", "dp"),
        P("tensor", "dp"),
        P(("dp", "tensor")),
        P(("dp", "tensor"), None),
    )
    out_specs = (
        P(("dp", "tensor"), None),
        P(("dp", "tensor"), None),
        P(("dp", "tensor")),
        P(("dp", "tensor")),
        P("dp", None, "tensor"),
        P(None, "tensor", "dp"),
        P("tensor", "dp"),
        P(("dp", "tensor")),
        P(("dp", "tensor")),
        P(("dp", "tensor")),
        P("dp", "tensor"),
        P("tensor", "dp"),
        P("tensor", "dp"),
        P(("dp", "tensor")),
    )
    return jax.shard_map(
        on_device, mesh=mesh, in_specs=in_specs, out_specs=out_specs, check_vma=False
    )
```

profile of v0, /device:TPU:0, one launch (start us, length us, event | category | flops | bytes accessed | tf_op | source)
XLA Modules:
  0.0 846.4 jit_solution(4965968082217313966)
XLA Ops:
  15.0 42.3 %all-reduce.15 = (f32[768]{0:T(1024)S(1)}, f32[768]{0:T(1024)S(1)}, f32[768]{0:T(1024)S(1)}, f32[768]{0:T(1024)S(1)}, f32[768]{0:T(1024)S(1)}) all-reduce(f32[768]{0:T(1024)S(1)} %dynamic-update-slice.1, f32[768]{0:T(1024)S(1)} %dynamic-update-slice, f32[768]{0:T(1024)S(1)} %dynamic-update-slice.2, ...), channel_id=1, replica_groups=mesh['dp'=8,'tensor'=4] {'dp','tensor'}, use_global_device_ids=true, to_apply=%add.1 | all-reduce | flops 3840 | bytes 30720
  57.3 2.2 fusion.49
  59.8 30.4 %all_gather.52 = bf16[2,3,64]{1,0,2:T(2,128)(2,1)S(1)} all-gather(bf16[2,3,8]{1,0,2:T(2,128)(2,1)S(1)} %copy.61), channel_id=1, replica_groups=mesh['dp'=8,'tensor'=4] {'dp'}, dimensions={2}, use_global_device_ids=true | all-gather | bytes 864 | tf_op jit(solution)/shard_map/all_gather | solution.py:51
  90.5 33.8 %all_gather.51 = bf16[768,3,192]{2,0,1:T(8,128)(2,1)S(1)} all-gather(bf16[96,3,192]{2,0,1:T(8,128)(2,1)S(1)} %copy-done.26), channel_id=1, replica_groups=mesh['dp'=8,'tensor'=4] {'dp'}, dimensions={0}, use_global_device_ids=true | all-gather | bytes 995328 | tf_op jit(solution)/shard_map/all_gather | solution.py:50
  125.0 31.0 %all_gather.53 = bf16[192,768]{0,1:T(8,128)(2,1)S(1)} all-gather(bf16[192,96]{0,1:T(8,128)(2,1)S(1)} %copy.65), channel_id=1, replica_groups=mesh['dp'=8,'tensor'=4] {'dp'}, dimensions={1}, use_global_device_ids=true | all-gather | bytes 331776 | tf_op jit(solution)/shard_map/all_gather | solution.py:52
  155.9 3.4 fusion.38
  159.8 34.5 %while.27 = (s32[]{:T(128)}, bf16[3,512,192]{1,2,0:T(8,128)(2,1)}, f32[3,3,512]{2,1,0:T(4,128)}, s32[3]{0:T(128)S(1)}, s32[1536]{0:T(1024)S(1)}, /*index=5*/s32[...) while((s32[]{:T(128)}, bf16[3,512,192]{1,2,0:T(8,128)(2,1)}, ...), condition=%wide.region_5.6_spmd, body=%wide.region_2.5_spmd.sunk | while | flops 633174528 | bytes 33499348 | solution.py:99
  161.6 2.0 fusion.117
  163.7 2.8 fusion.118
  166.4 3.5 fusion.119
  173.1 2.0 fusion.117
  175.1 2.8 fusion.118
  177.9 3.5 fusion.119
  184.6 2.0 fusion.117
  186.7 2.8 fusion.118
  189.4 3.5 fusion.119
  195.6 3.0 fusion.67
  199.3 46.7 %reduce-scatter.13.cloned.1.call-done = f32[384,768]{1,0:T(8,128)} async-done(((f32[1536,768]{1,0:T(8,128)}), f32[384,768]{1,0:T(8,128)}) %reduce-scatter.13.cloned.1.call-update) | async-done | bytes 1179664 | tf_op jit(solution)/shard_map/reduce_scatter | solution.py:102
  250.3 26.2 %all_gather.59 = bf16[12,64]{0,1:T(8,128)(2,1)S(1)} all-gather(bf16[12,8]{0,1:T(8,128)(2,1)S(1)} %copy-done.41), channel_id=1, replica_groups=mesh['dp'=8,'tensor'=4] {'dp'}, dimensions={1}, use_global_device_ids=true | all-gather | bytes 1728 | tf_op jit(solution)/shard_map/all_gather | solution.py:54
  276.7 6.2 fusion.68
  282.8 33.9 %all-gather.13.cloned.1.call-done = bf16[768,768]{0,1:T(8,128)(2,1)} async-done(((bf16[768,96]{0,1:T(8,128)(2,1)}), bf16[768,768]{0,1:T(8,128)(2,1)}) %all-gather.13.cloned.1.call-update) | async-done | bytes 1179664 | tf_op jit(solution)/shard_map/all_gather | solution.py:55
  316.8 24.1 %all-gather.15.cloned.1.call-done = bf16[1536,768]{1,0:T(8,128)(2,1)} async-done(((bf16[384,768]{1,0:T(8,128)(2,1)}), bf16[1536,768]{1,0:T(8,128)(2,1)}) %all-gather.15.cloned.1.call-update) | async-done | bytes 2359312 | tf_op jit(solution)/shard_map/all_gather | solution.py:121
  340.9 16.0 %convert_reduce_fusion = (f32[768]{0:T(1024)}, bf16[1536,768]{1,0:T(8,128)(2,1)S(1)}, f32[1536,768]{1,0:T(8,128)}) fusion(f32[1536,768]{1,0:T(8,128)} %fusion.68, f32[768]{0:T(1024)S(1)} %reshape.224, bf16[1536,768]{1,0:T(8,128)(2,1)} %all-gather.15.cloned.1.call-done, bf16[768,768]{0,1:T(8,128)(2,1)} %all-gather.13.cloned.1.call-done), kind=kOutput, calls=%fused_computation.42 | convolution fusion | flops 1900412160 | bytes 15341568 | tf_op jit(solution)/shard_map/ld,fd->lf/dot_general | solution.py:21
  358.3 3.6 convolution_convert_fusion
  361.9 33.1 %reduce-scatter.17.cloned.1.call-done = bf16[384,768]{1,0:T(8,128)(2,1)} async-done(((bf16[1536,768]{1,0:T(8,128)(2,1)}), bf16[384,768]{1,0:T(8,128)(2,1)}) %reduce-scatter.17.cloned.1.call-update) | async-done | bytes 589840 | tf_op jit(solution)/shard_map/reduce_scatter | solution.py:127
  395.0 2.2 fusion.53
  399.8 1.7 convert_reduce_fusion.6
  401.6 24.1 %all-gather.17.cloned.1.call-done = bf16[1536,768]{1,0:T(8,128)(2,1)} async-done(((bf16[384,768]{1,0:T(8,128)(2,1)}), bf16[1536,768]{1,0:T(8,128)(2,1)}) %all-gather.17.cloned.1.call-update) | async-done | bytes 2359312 | tf_op jit(solution)/shard_map/all_gather | solution.py:139
  425.7 3.8 convolution_bitcast_fusion
  429.8 3.5 convolution_convert_fusion.2
  433.2 106.5 %while.28 = (s32[]{:T(128)}, f32[1536,3,64]{0,2,1:T(8,128)}, f32[1536,3,64]{0,2,1:T(8,128)S(1)}, bf16[3,512,3,64]{1,3,2,0:T(8,128)(2,1)}, s32[3]{0:T(128)S(1)}, ...) while((s32[]{:T(128)}, f32[1536,3,64]{0,2,1:T(8,128)}, ...), condition=%wide.region_15.16_spmd.clone, body=%wide.region_13.15_spmd.clone.sunk | while | flops 1533540864 | bytes 150903440 | solution.py:166
  439.7 2.4 fusion.129
  442.1 7.2 multiply_reduce_fusion.3
  449.3 9.5 %multiply_convert_fusion.3 = bf16[3,512,1536]{2,1,0:T(8,128)(2,1)} fusion(f32[3,512,1536]{2,1,0:T(8,128)} %get-tuple-element.446, f32[3,512,1536]{2,1,0:T(8,128)} %copy-done, f32[3,512]{1,0:T(4,128)S(1)} %get-tuple-element.447), kind=kLoop, calls=%fused_computation.15.clone.1 | loop fusion | flops 7077888 | bytes 23599104 | tf_op jit(solution)/shard_map/while/body/eval_jaxpr/convert_element_type | solution.py:157
  458.7 5.0 fusion.131
  465.6 2.1 fusion.130
  475.3 2.4 fusion.129
  477.6 7.2 multiply_reduce_fusion.3
  484.8 9.4 %multiply_convert_fusion.3 = bf16[3,512,1536]{2,1,0:T(8,128)(2,1)} fusion(f32[3,512,1536]{2,1,0:T(8,128)} %get-tuple-element.446, f32[3,512,1536]{2,1,0:T(8,128)} %copy-done, f32[3,512]{1,0:T(4,128)S(1)} %get-tuple-element.447), kind=kLoop, calls=%fused_computation.15.clone.1 | loop fusion | flops 7077888 | bytes 23599104 | tf_op jit(solution)/shard_map/while/body/eval_jaxpr/convert_element_type | solution.py:157
  494.3 5.0 fusion.131
  501.1 2.1 fusion.130
  510.8 2.3 fusion.129
  513.1 7.2 multiply_reduce_fusion.3
  520.3 9.4 %multiply_convert_fusion.3 = bf16[3,512,1536]{2,1,0:T(8,128)(2,1)} fusion(f32[3,512,1536]{2,1,0:T(8,128)} %get-tuple-element.446, f32[3,512,1536]{2,1,0:T(8,128)} %copy-done, f32[3,512]{1,0:T(4,128)S(1)} %get-tuple-element.447), kind=kLoop, calls=%fused_computation.15.clone.1 | loop fusion | flops 7077888 | bytes 23599104 | tf_op jit(solution)/shard_map/while/body/eval_jaxpr/convert_element_type | solution.py:157
  529.7 5.0 fusion.131
  536.6 2.1 fusion.130
  539.7 2.5 copy.67
  542.2 2.6 stack_reshape.12
  547.2 3.6 bitcast_convert_fusion
  551.5 4.5 multiply_convert_fusion.1
  557.4 3.5 convolution_convert_fusion.1
  561.0 5.8 fusion.70
  566.9 6.3 fusion.69
  574.6 5.2 fusion.36
  586.8 37.1 %all-reduce.16 = (f32[2,3,64]{2,1,0:T(4,128)S(1)}, f32[12,64]{1,0:T(8,128)S(1)}) all-reduce(f32[2,3,64]{2,1,0:T(4,128)S(1)} %reshape.222, f32[12,64]{1,0:T(8,128)} %reshape.223), channel_id=9, replica_groups=mesh['dp'=8,'tensor'=4] {'dp'}, use_global_device_ids=true, to_apply=%region_25.26.clone | all-reduce | flops 1152 | bytes 9216
  625.3 1.6 copy.76
  627.0 2.1 convert_reduce_fusion.2
  629.8 2.4 fusion.54
  632.2 3.3 add_add_fusion.2
  635.5 38.0 %all-reduce.14 = (f32[768]{0:T(1024)S(1)}, f32[768]{0:T(1024)S(1)}, f32[768]{0:T(1024)S(1)}, f32[768]{0:T(1024)S(1)}, f32[768]{0:T(1024)S(1)}, /*index=5*/f32[768]{0:T(1024)S(1)}, f32[768]{0:T(1024)S(1)}) all-reduce(f32[768]{0:T(1024)} %dynamic-update-slice.5, ...), channel_id=1, replica_groups=mesh['dp'=8,'tensor'=4] {'dp','tensor'}, use_global_device_ids=true, to_apply=%add.5 | all-reduce | flops 5376 | bytes 43008
  677.0 2.0 add_convert_fusion.1
  679.0 14.2 %reduce-scatter.25.cloned.1.call-done = f32[768,96]{0,1:T(8,128)} async-done(((f32[768,768]{0,1:T(8,128)}), f32[768,96]{0,1:T(8,128)}) %reduce-scatter.25.cloned.1.call-update) | async-done | bytes 294928 | tf_op jit(solution)/shard_map/reduce_scatter | solution.py:197
  693.1 72.9 %reduce-scatter.23.cloned.1.call-done = f32[96,768]{1,0:T(8,128)} async-done(((f32[768,768]{1,0:T(8,128)}), f32[96,768]{1,0:T(8,128)}) %reduce-scatter.23.cloned.1.call-update) | async-done | bytes 294928 | tf_op jit(solution)/shard_map/reduce_scatter | solution.py:195
  766.0 72.6 %reduce-scatter.21.cloned.1.call-done = f32[96,3,192]{2,0,1:T(8,128)} async-done(((f32[768,3,192]{2,0,1:T(8,128)}), f32[96,3,192]{2,0,1:T(8,128)}) %reduce-scatter.21.cloned.1.call-update) | async-done | bytes 221200 | tf_op jit(solution)/shard_map/reduce_scatter | solution.py:192
  (268 shorter events, 64.6 us)
Async XLA Ops:
  8.0 51.6 %copy-start.42 = (bf16[2,3,8]{2,0,1:T(2,128)(2,1)S(1)}, bf16[2,3,8]{2,0,1:T(2,128)(2,1)}, u32[]{:S(2)}) copy-start(bf16[2,3,8]{2,0,1:T(2,128)(2,1)} %param.24) | copy-start | bytes 292
  8.0 51.7 %copy-start.23 = (s32[1,1536]{1,0:T(1,128)S(1)}, s32[1,1536]{1,0:T(1,128)}, u32[]{:S(2)}) copy-start(s32[1,1536]{1,0:T(1,128)} %param.20) | copy-start | bytes 18436
  8.0 82.3 %copy-start.33 = (bf16[192,96]{1,0:T(8,128)(2,1)S(1)}, bf16[192,96]{1,0:T(8,128)(2,1)}, u32[]{:S(2)}) copy-start(bf16[192,96]{1,0:T(8,128)(2,1)} %param.25) | copy-start | bytes 110596
  8.0 82.4 %copy-start.26 = (bf16[96,3,192]{2,0,1:T(8,128)(2,1)S(1)}, bf16[96,3,192]{2,0,1:T(8,128)(2,1)}, u32[]{:S(2)}) copy-start(bf16[96,3,192]{2,0,1:T(8,128)(2,1)} %param.23) | copy-start | bytes 331780
  8.1 147.9 %all-gather.7.cloned.1.call-start = ((), (), s32[]{:S(2)}) async-start(), calls=%async_computation.8 | async-start | bytes 2949120 | tf_op jit(solution)/shard_map/all_gather | solution.py:66
  9.4 50.4 %copy-start.29 = (f32[384]{0:T(512)}, f32[384]{0:T(512)S(1)}, u32[]{:S(2)}) copy-start(f32[384]{0:T(512)S(1)} %broadcast_multiply_fusion.1) | copy-start | bytes 4612
  10.7 3.4 copy-start.38
  10.8 49.0 %copy-start.34 = (f32[384]{0:T(512)}, f32[384]{0:T(512)S(1)}, u32[]{:S(2)}) copy-start(f32[384]{0:T(512)S(1)} %fusion.58) | copy-start | bytes 4612
  57.3 2.4 copy-start.31
  59.5 186.5 %reduce-scatter.13.cloned.1.call-start = ((), (), s32[]{:S(2)}) async-start(), calls=%async_computation.9 | async-start | bytes 5898240 | tf_op jit(solution)/shard_map/reduce_scatter | solution.py:102
  124.3 35.0 %copy-start.11 = (bf16[768,3,192]{2,0,1:T(8,128)(2,1)}, bf16[768,3,192]{2,0,1:T(8,128)(2,1)S(1)}, u32[]{:S(2)}) copy-start(bf16[768,3,192]{2,0,1:T(8,128)(2,1)S(1)} %all_gather.51) | copy-start | bytes 2654212
  155.9 39.7 %copy-start.13 = (bf16[192,768]{0,1:T(8,128)(2,1)}, bf16[192,768]{0,1:T(8,128)(2,1)S(1)}, u32[]{:S(2)}) copy-start(bf16[192,768]{0,1:T(8,128)(2,1)S(1)} %all_gather.53) | copy-start | bytes 884740
  194.3 4.3 copy-start.6
  195.6 3.0 copy-start.21
  198.6 47.4 %copy-start.4 = (bf16[384,768]{1,0:T(8,128)(2,1)S(1)}, bf16[384,768]{1,0:T(8,128)(2,1)}, u32[]{:S(2)}) copy-start(bf16[384,768]{1,0:T(8,128)(2,1)} %param.19) | copy-start | bytes 1769476
  198.6 78.0 %all-gather.11.cloned.1.call-start = ((), (), s32[]{:S(2)}) async-start(), calls=%async_computation.11 | async-start | bytes 1327104 | tf_op jit(solution)/shard_map/all_gather | solution.py:53
  199.2 77.5 %all-gather.9.cloned.1.call-start = ((), (), s32[]{:S(2)}) async-start(), calls=%async_computation.10 | async-start | bytes 2949120 | tf_op jit(solution)/shard_map/all_gather | solution.py:106
  247.5 2.8 copy-start.41
  248.9 67.9 %all-gather.13.cloned.1.call-start = ((), (), s32[]{:S(2)}) async-start(), calls=%async_computation.12 | async-start | bytes 1327104 | tf_op jit(solution)/shard_map/all_gather | solution.py:55
  249.5 91.4 %all-gather.15.cloned.1.call-start = ((), (), s32[]{:S(2)}) async-start(), calls=%async_computation.14 | async-start | bytes 2949120 | tf_op jit(solution)/shard_map/all_gather | solution.py:121
  250.2 144.8 %reduce-scatter.17.cloned.1.call-start = ((), (), s32[]{:S(2)}) async-start(), calls=%async_computation.15 | async-start | bytes 2949120 | tf_op jit(solution)/shard_map/reduce_scatter | solution.py:127
  276.7 64.2 %copy-start.39 = (f32[768]{0:T(1024)}, f32[768]{0:T(1024)S(1)}, u32[]{:S(2)}) copy-start(f32[768]{0:T(1024)S(1)} %reshape.224) | copy-start | bytes 9220
  340.9 17.4 %copy-start.44 = (bf16[768,768]{1,0:T(8,128)(2,1)S(1)}, bf16[768,768]{1,0:T(8,128)(2,1)}, u32[]{:S(2)}) copy-start(bf16[768,768]{1,0:T(8,128)(2,1)} %all-gather.11.cloned.1.call-done) | copy-start | bytes 3538948
  361.9 37.9 %copy-start.10 = (bf16[384,768]{1,0:T(8,128)(2,1)S(1)}, bf16[384,768]{1,0:T(8,128)(2,1)}, u32[]{:S(2)}) copy-start(bf16[384,768]{1,0:T(8,128)(2,1)} %param.33) | copy-start | bytes 1769476
  361.9 63.8 %all-gather.17.cloned.1.call-start = ((), (), s32[]{:S(2)}) async-start(), calls=%async_computation.16 | async-start | bytes 2949120 | tf_op jit(solution)/shard_map/all_gather | solution.py:139
  398.8 2.8 copy-start.36
  401.5 223.8 %reduce-scatter.27.cloned.1.call-start = ((), (), s32[]{:S(2)}) async-start(), calls=%async_computation.21 | async-start | bytes 884736
  429.5 197.4 %reduce-scatter.19.cloned.1.call-start = ((), (), s32[]{:S(2)}) async-start(), calls=%async_computation.17 | async-start | bytes 2949120 | tf_op jit(solution)/shard_map/reduce_scatter | solution.py:182
  433.2 3.2 copy-start.45
  433.3 3.8 copy-start.27
  442.1 7.2 copy-start
  458.7 5.2 copy-start.1
  458.7 5.3 copy-start.24
  465.6 2.2 copy-start.25
  465.6 3.2 copy-start.28
  465.6 3.2 copy-start.46
  468.8 3.2 copy-start.45
  468.8 3.9 copy-start.27
  477.6 7.2 copy-start
  494.3 5.1 copy-start.1
  494.3 5.3 copy-start.24
  501.1 3.2 copy-start.28
  501.1 3.2 copy-start.46
  504.3 3.2 copy-start.45
  504.3 3.9 copy-start.27
  513.1 7.2 copy-start
  529.7 5.1 copy-start.1
  529.7 5.3 copy-start.24
  536.5 3.2 copy-start.28
  536.6 3.2 copy-start.46
  542.2 5.0 copy-start.12
  544.8 2.4 copy-start.19
  550.9 126.1 %reduce-scatter.15.cloned.1.call-start = ((), (), s32[]{:S(2)}) async-start(), calls=%async_computation.13 | async-start | bytes 2949120 | tf_op jit(solution)/shard_map/reduce_scatter | solution.py:112
  551.5 5.9 copy-start.43
  560.9 132.2 %reduce-scatter.25.cloned.1.call-start = ((), (), s32[]{:S(2)}) async-start(), calls=%async_computation.20 | async-start | bytes 2654208 | tf_op jit(solution)/shard_map/reduce_scatter | solution.py:197
  566.8 199.2 %reduce-scatter.23.cloned.1.call-start = ((), (), s32[]{:S(2)}) async-start(), calls=%async_computation.19 | async-start | bytes 2654208 | tf_op jit(solution)/shard_map/reduce_scatter | solution.py:195
  573.2 265.4 %reduce-scatter.21.cloned.1.call-start = ((), (), s32[]{:S(2)}) async-start(), calls=%async_computation.18 | async-start | bytes 2654208 | tf_op jit(solution)/shard_map/reduce_scatter | solution.py:192
  579.8 47.2 %copy-start.5 = (bf16[384,768]{1,0:T(8,128)(2,1)S(1)}, bf16[384,768]{1,0:T(8,128)(2,1)}, u32[]{:S(2)}) copy-start(bf16[384,768]{1,0:T(8,128)(2,1)} %param.19) | copy-start | bytes 1769476
  579.8 47.2 %copy-start.30 = (f32[384]{0:T(512)S(1)}, f32[384]{0:T(512)}, u32[]{:S(2)}) copy-start(f32[384]{0:T(512)} %copy-done.29) | copy-start | bytes 4612
  579.8 47.2 %copy-start.32 = (f32[768]{0:T(1024)S(1)}, f32[768]{0:T(1024)}, u32[]{:S(2)}) copy-start(f32[768]{0:T(1024)} %copy-done.31) | copy-start | bytes 9220
  579.8 50.0 %copy-start.35 = (f32[384]{0:T(512)S(1)}, f32[384]{0:T(512)}, u32[]{:S(2)}) copy-start(f32[384]{0:T(512)} %copy-done.34) | copy-start | bytes 4612
  579.8 52.4 %copy-start.8 = (f32[384,768]{1,0:T(8,128)S(1)}, f32[384,768]{1,0:T(8,128)}, u32[]{:S(2)}) copy-start(f32[384,768]{1,0:T(8,128)} %copy-done.7) | copy-start | bytes 3538948
  579.8 52.4 %copy-start.37 = (f32[384]{0:T(512)S(1)}, f32[384]{0:T(512)}, u32[]{:S(2)}) copy-start(f32[384]{0:T(512)} %copy-done.36) | copy-start | bytes 4612
  626.9 5.2 copy-start.9
  (17 other events, 22.0 us)
Sparse Core Ops, SparseCore 0:
  59.6 23.9 all-gather.6
  198.8 47.1 reduce-scatter.12
  401.6 24.0 all-gather.16
Sparse Core Ops, SparseCore 1:
  201.5 40.6 all-gather.10
  249.0 23.9 all-gather.8
  275.2 41.5 all-gather.12
  318.4 22.4 all-gather.14
  362.0 33.0 reduce-scatter.16
  429.6 62.5 reduce-scatter.26
  551.0 33.0 reduce-scatter.18
  586.4 33.0 reduce-scatter.14
  623.8 69.3 reduce-scatter.24
  697.6 68.3 reduce-scatter.22
  770.3 68.2 reduce-scatter.20
where the time goes:
time: 856 us; the launch traced here: 846 us
  waiting for transfers between devices  323 us (38%)
  blocking collectives  239 us (28%)
  matrix products  135 us (16%)
  other arithmetic  77.1 us (9%)
  local copies, waits for them, and re-layouts  43.5 us (5%)
  between operations  17.1 us (2%)
  loops' own time  10.2 us (1%)
    unnamed x3, blocking collectives  117 us
    dot_general x28, matrix products, contract(): return jnp.einsum(pattern, left, right, preferred_element_type=jnp.float32)  115 us
    reduce_scatter x1, waiting for transfers between devices, on_device(): lax.psum_scatter(grad_fc1, 'dp', scatter_dimension=0, tiled=True)  72.9 us
    reduce_scatter x1, waiting for transfers between devices, on_device(): lax.psum_scatter(grad_in_w, 'dp', scatter_dimension=0, tiled=True)  72.6 us
    reduce_scatter x1, waiting for transfers between devices, on_device(): lax.psum_scatter(attn_partial, 'tensor', scatter_dimension=0, tiled=True)  46.7 us
    all_gather x1, waiting for transfers between devices, on_device(): lax.all_gather(fc2_weight, 'dp', axis=1, tiled=True)  33.9 us
    all_gather x1, blocking collectives, on_device(): lax.all_gather(in_weight, 'dp', axis=0, tiled=True)  33.8 us
    reduce_scatter x1, waiting for transfers between devices, on_device(): lax.psum_scatter(contract('lf,df->ld', grad_hidden, fc1_full).astype(jnp....  33.1 us
  transfers between devices with their start and end apart: 14, of which 8 were waited for; matrix products, arithmetic and copies ran while one was open for 20% of the time, Pallas kernels for 0%

commit v1 on v0

v1 whole, which is shorter than its diff:
```python
import functools

import jax
import jax.numpy as jnp
from jax import lax
from jax.experimental import pallas as pl
from jax.experimental.pallas import tpu as pltpu
from jax.sharding import PartitionSpec as P

HD = 64
BF = jnp.bfloat16
F32 = jnp.float32
VMEM_BYTES = 62 << 20
BLOCK = 256
CHUNKS = 3
LANE_GAP = 256


def layer_norm(row_block, norm_gain, norm_shift):
    row_mean = jnp.mean(row_block, axis=-1, keepdims=True)
    centred = row_block - row_mean
    row_var = jnp.mean(centred * centred, axis=-1, keepdims=True)
    return centred * lax.rsqrt(row_var + 1e-05) * norm_gain + norm_shift


def layer_norm_back(row, grad, gain):
    mean = jnp.mean(row, axis=-1, keepdims=True)
    centred = row - mean
    scale = lax.rsqrt(jnp.mean(centred * centred, axis=-1, keepdims=True) + 1e-05)
    unit = centred * scale
    scaled = grad * gain
    back = scale * (
        scaled
        - jnp.mean(scaled, axis=-1, keepdims=True)
        - unit * jnp.mean(scaled * unit, axis=-1, keepdims=True)
    )
    return back, unit


def dot_nn(left, right):
    return jnp.dot(left, right, preferred_element_type=F32)


def dot_nt(left, right):
    return lax.dot_general(left, right, (((1,), (1,)), ((), ())), preferred_element_type=F32)


def dot_tn(left, right):
    return lax.dot_general(left, right, (((0,), (0,)), ((), ())), preferred_element_type=F32)


def column_sum(block):
    return jnp.sum(block, axis=0, keepdims=True)


def head_part(block, head):
    lanes = lax.broadcasted_iota(jnp.int32, block.shape, 1)
    inside = (lanes >= head * HD) & (lanes < (head + 1) * HD)
    return jnp.where(inside, block, jnp.zeros_like(block))


def rows_at(start, size):
    return pl.ds(pl.multiple_of(start, 128), size)


class Links:
    def __init__(self, num_dp, send_sems, recv_sems):
        self.num_dp, self.num_far = num_dp, num_dp // 2
        self.dp, self.tensor = lax.axis_index("dp"), lax.axis_index("tensor")
        self.send_sems, self.recv_sems, self.made, self.done = send_sems, recv_sems, [], []
        self.sibling = (self.dp, self.tensor ^ 1)
        self.across = (self.dp, self.tensor ^ 2)
        self.corner = (self.dp, self.tensor ^ 3)
        self.beside = (self.dp ^ 1, self.tensor)
        self.others = [(lax.rem(self.dp + step, num_dp), self.tensor) for step in range(1, num_dp)]

    def far(self, step):
        return lax.rem(self.dp + 2 * step, self.num_dp)

    def far_from(self, step):
        return lax.rem(self.dp + self.num_dp - 2 * step, self.num_dp)

    def copy(self, src, dst, device):
        at = len(self.made)
        made = pltpu.make_async_remote_copy(
            src_ref=src,
            dst_ref=dst,
            send_sem=self.send_sems.at[at],
            recv_sem=self.recv_sems.at[at],
            device_id=device,
            device_id_type=pl.DeviceIdType.MESH,
        )
        self.made.append(made)
        return made

    def greet(self, devices):
        barrier = pltpu.get_barrier_semaphore()
        for device in devices:
            pl.semaphore_signal(
                barrier, inc=1, device_id=device, device_id_type=pl.DeviceIdType.MESH
            )
        pl.semaphore_wait(barrier, len(devices))

    def sent(self, copies):
        for made in copies:
            made.wait_send()
            self.done.append(made)

    def finish(self):
        for made in self.made:
            if not any(made is other for other in self.done):
                made.wait_send()


class WeightSpread:
    def __init__(self, links, shard, full, halves):
        self.links, self.shard, self.full, self.halves = links, shard, full, halves
        columns = shard.shape[-1] // halves

        def part(ref, half):
            return ref.at[:, pl.ds(half * columns, columns)]

        def place(origin, half):
            return full.at[origin, :, pl.ds(half * columns, columns)]

        self.first, self.second = {}, {}
        for half in range(halves):
            for step in range(1, links.num_far):
                self.first[half, step] = links.copy(
                    part(shard, half), place(links.dp, half), (links.far(step), links.tensor)
                )
            self.second[half, 0] = links.copy(
                part(shard, half), place(links.dp, half), links.beside
            )
            for step in range(1, links.num_far):
                spot = place(links.far_from(step), half)
                self.second[half, step] = links.copy(spot, spot, links.beside)

    def begin(self):
        for made in self.first.values():
            made.start()
        for half in range(self.halves):
            self.second[half, 0].start()
        self.full[self.links.dp] = self.shard[...]

    def forward(self, half):
        for step in range(1, self.links.num_far):
            self.first[half, step].wait_recv()
            self.second[half, step].start()

    def end(self):
        for made in self.second.values():
            made.wait_recv()


class RowSum:
    def __init__(self, links, part, side, home, far):
        self.links, self.part = links, part
        self.side, self.home, self.far = side, home, far
        self.block = part.shape[0] // 4
        self.rows = self.block // CHUNKS
        me = links.tensor
        cuts = [self.cut(chunk) for chunk in range(CHUNKS)]
        self.side_in = [
            links.copy(part.at[self.of(me ^ 3, chunk)], side.at[cuts[chunk]], links.sibling)
            for chunk in range(CHUNKS)
        ]
        self.home_in = [
            links.copy(part.at[self.of(me ^ 1, chunk)], home.at[cuts[chunk]], links.sibling)
            for chunk in range(CHUNKS)
        ]
        self.far_in = [
            links.copy(side.at[cuts[chunk]], far.at[cuts[chunk]], links.across)
            for chunk in range(CHUNKS)
        ]

    def cut(self, chunk):
        return pl.ds(chunk * self.rows, self.rows)

    def of(self, member, chunk):
        return rows_at(member * self.block + chunk * self.rows, self.rows)

    def begin_side(self):
        for made in self.side_in:
            made.start()

    def begin_home(self):
        for made in self.home_in:
            made.start()

    def pass_on(self, chunk):
        cut = self.cut(chunk)
        self.side_in[chunk].wait_recv()
        mine = self.part[self.of(self.links.tensor ^ 2, chunk), :]
        self.side[cut, :] = (mine.astype(F32) + self.side[cut, :].astype(F32)).astype(BF)
        self.far_in[chunk].start()

    def total(self, chunk):
        cut = self.cut(chunk)
        self.home_in[chunk].wait_recv()
        self.far_in[chunk].wait_recv()
        return (
            self.part[self.of(self.links.tensor, chunk), :].astype(F32)
            + self.home[cut, :].astype(F32)
            + self.far[cut, :].astype(F32)
        )


class RowSpread:
    def __init__(self, links, own, gathered):
        self.block = own.shape[0]
        self.rows = self.block // CHUNKS
        self.own, self.gathered, self.links = own, gathered, links
        me = links.tensor
        self.across_in, self.sibling_in, self.corner_in = [], [], []
        for chunk in range(CHUNKS):
            source, place = own.at[self.cut(chunk)], gathered.at[self.of(me, chunk)]
            self.across_in.append(links.copy(source, place, links.across))
            self.sibling_in.append(links.copy(source, place, links.sibling))
        for chunk in range(CHUNKS):
            place = gathered.at[self.of(me ^ 2, chunk)]
            self.corner_in.append(links.copy(place, place, links.sibling))

    def cut(self, chunk):
        return pl.ds(chunk * self.rows, self.rows)

    def of(self, member, chunk):
        return rows_at(member * self.block + chunk * self.rows, self.rows)

    def give(self, chunk):
        self.across_in[chunk].start()
        self.sibling_in[chunk].start()
        self.gathered[self.of(self.links.tensor, chunk), :] = self.own[self.cut(chunk), :]

    def hand_over(self, chunk):
        self.across_in[chunk].wait_recv()
        self.corner_in[chunk].start()

    def await_sibling(self):
        for made in self.sibling_in:
            made.wait_recv()

    def await_corner(self):
        for made in self.corner_in:
            made.wait_recv()


class GradScatter:
    def __init__(self, links, grads, beside, landed, result):
        self.links, self.grads, self.beside = links, grads, beside
        self.landed, self.result = landed, result
        self.slab = beside.shape[1]
        self.beside_in, self.far_in = {}, {}
        for step in range(links.num_far):
            target = links.far(step)
            self.beside_in[step] = links.copy(
                grads.at[target ^ 1], beside.at[step], links.beside
            )
            if step:
                self.far_in[step] = links.copy(
                    beside.at[step], landed.at[step], (target, links.tensor)
                )

    def begin(self):
        for step in range(1, self.links.num_far + 1):
            self.beside_in[step % self.links.num_far].start()

    def pass_on(self, step):
        self.beside_in[step].wait_recv()
        mine = self.grads[self.links.far(step)]
        self.beside[step] = (mine.astype(F32) + self.beside[step].astype(F32)).astype(BF)
        self.far_in[step].start()

    def end(self):
        self.beside_in[0].wait_recv()
        total = self.grads[self.links.dp].astype(F32) + self.beside[0].astype(F32)
        for step in range(1, self.links.num_far):
            self.far_in[step].wait_recv()
            total = total + self.landed[step].astype(F32)
        self.result[...] = total


class Refs:
    def __init__(self, names, refs):
        for name, ref in zip(names, refs, strict=True):
            setattr(self, name, ref)


def flat_weight(full, wide):
    count, slab, width = full.shape
    if slab % 16 == 0:
        return full[...].reshape(count * slab, width)
    for at in range(count):
        wide[at * slab : (at + 1) * slab, :] = full[at].astype(F32)
    return wide[...].astype(BF)


def split_rows(value, grads, start, wide):
    count, slab, width = grads.shape
    rows = value.shape[0]
    if slab % 16 == 0:
        grads[pl.ds(start // slab, rows // slab)] = value.astype(BF).reshape(
            rows // slab, slab, width
        )
        return
    wide[0:rows, :] = value
    for at in range(rows // slab):
        grads[start // slab + at] = wide[at * slab : (at + 1) * slab, :].astype(BF)


def layer_kernel(num_dp, names, *refs):
    r = Refs(names, refs)
    links = Links(num_dp, r.send_sems, r.recv_sems)
    me, dp = links.tensor, links.dp
    block, width = r.frames.shape
    length = 4 * block
    num_blocks = length // BLOCK
    heads_width = width // 4
    heads = heads_width // HD
    qkv = 3 * heads_width
    upper = me // 2
    parts = 2 * CHUNKS

    links.greet(links.others + [links.sibling, links.across, links.corner])

    small_dp = [
        links.copy(r.small_mine, r.small_dp.at[at], other) for at, other in enumerate(links.others)
    ]
    small_group = [
        links.copy(r.small_sum, r.small_group.at[at], device)
        for at, device in enumerate((links.sibling, links.across, links.corner))
    ]
    frame_rows = RowSpread(links, r.frames, r.rows_all)
    given_rows = RowSpread(links, r.cotangent, r.given_all)
    spread_a = WeightSpread(links, r.shard_a, r.full_a, 2)
    spread_b = WeightSpread(links, r.shard_b, r.full_b, 2)
    spread_c = WeightSpread(links, r.shard_c, r.full_c, 2)

    placed = pltpu.roll(r.small[0:6, :], (dp * 4 + me) * (width // (4 * num_dp)), 1)
    r.small_mine[0:6, :] = placed
    r.small_mine[6:8, :] = pltpu.roll(r.small[6:8, :], dp * (HD // num_dp), 1)
    for made in small_dp:
        made.start()
    for chunk in range(CHUNKS):
        frame_rows.give(chunk)
    spread_a.begin()
    for chunk in range(CHUNKS):
        given_rows.give(chunk)
    spread_b.begin()
    spread_c.begin()

    ids = r.seg_row[0:1, :].astype(F32)
    r.seg_wide[...] = jnp.transpose(jnp.broadcast_to(ids, (128, length)))

    total = r.small_mine[...]
    for at, made in enumerate(small_dp):
        made.wait_recv()
        total = total + r.small_dp[at]
    r.small_sum[...] = total
    for made in small_group:
        made.start()
    for at, made in enumerate(small_group):
        made.wait_recv()
        total = total + jnp.where(
            lax.broadcasted_iota(jnp.int32, total.shape, 0) < 6, r.small_group[at], 0.0
        )
    r.vecs[...] = total
    gain_one, shift_one, gain_two, shift_two, bias_out, bias_fc2 = range(6)

    def vec(at):
        return r.vecs[at : at + 1, :]

    for chunk in range(CHUNKS):
        frame_rows.hand_over(chunk)
    spread_a.forward(0)
    spread_a.forward(1)
    frame_rows.await_sibling()
    frame_rows.await_corner()
    spread_a.end()
    links.sent(frame_rows.corner_in)

    @pl.loop(0, num_blocks)
    def project(at):
        rows = rows_at(at * BLOCK, BLOCK)
        low = layer_norm(
            r.rows_all[rows, :].astype(F32), vec(gain_one), vec(shift_one)
        ).astype(BF)
        r.normed[rows, :] = low
        made = dot_nn(low, flat_weight(r.full_a, r.wide)[:, :qkv])
        made_query = (made[:, :heads_width] + r.vecs[7:8, 0:heads_width]).astype(BF)
        r.query[rows, :] = made_query * jnp.asarray(0.125, BF)
        r.keys[rows, :] = made[:, heads_width : 2 * heads_width].astype(BF)
        shift = r.vecs[7:8, LANE_GAP : LANE_GAP + heads_width]
        made_values = (made[:, 2 * heads_width :] + shift).astype(BF)
        r.values[rows, :] = made_values
        r.turned[:, rows] = jnp.transpose(made_values)

    sum_one = RowSum(links, r.part_one, r.side_one, r.home_one, r.far_one)
    spread_two = RowSpread(links, r.normed_own, r.normed_two)

    @pl.loop(0, num_blocks)
    def attend(at):
        spot = lax.rem(at + (1 - upper) * (num_blocks // 2), num_blocks)
        rows = rows_at(spot * BLOCK, BLOCK)
        asked = r.query[rows, :]
        keys_ids = jnp.concatenate([r.seg_wide[...]] * (BLOCK // 128), axis=1)
        query_ids = r.seg_row[0:1, rows].astype(F32)
        r.mask[...] = jnp.where(keys_ids == query_ids, 0.0, -1e30)
        made = []
        for head in range(heads):
            scores = dot_nt(r.keys[...], head_part(asked, head)) + r.mask[...]
            top = jnp.max(scores, axis=0, keepdims=True)
            weights = jnp.exp(scores - top)
            whole = column_sum(weights)
            mixed = dot_nn(r.turned[head * HD : (head + 1) * HD, :], weights.astype(BF))
            made.append(mixed / whole)
            r.stats[spot, head : head + 1, :] = top + jnp.log(whole)
        out = jnp.transpose(jnp.concatenate(made, axis=0)).astype(BF)
        r.mixed[rows, :] = out
        r.part_one[rows, :] = dot_nt(out, flat_weight(r.full_a, r.wide)[:, qkv:]).astype(BF)

        @pl.when(at == 0)
        def early():
            given_rows.hand_over(0)
            spread_b.forward(0)

        @pl.when(at == 1)
        def second():
            given_rows.hand_over(1)
            given_rows.hand_over(2)

        @pl.when(at == 2)
        def third():
            sum_one.begin_side()
            spread_b.forward(1)

        @pl.when(at == 3)
        def fourth():
            for chunk in range(CHUNKS):
                sum_one.pass_on(chunk)

        @pl.when(at == 4)
        def fifth():
            spread_c.forward(0)

    sum_one.begin_home()
    spread_c.forward(1)
    for chunk in range(CHUNKS):
        cut = sum_one.cut(chunk)
        row = r.frames[cut, :].astype(F32) + (sum_one.total(chunk) + vec(bias_out))
        r.middle[cut, :] = row
        r.normed_own[cut, :] = layer_norm(row, vec(gain_two), vec(shift_two)).astype(BF)
        spread_two.give(chunk)
    links.sent(sum_one.far_in)
    given_rows.await_sibling()
    given_rows.await_corner()
    spread_b.end()
    spread_c.end()

    sum_two = RowSum(links, r.part_two, r.side_two, r.home_two, r.far_two)
    sum_three = RowSum(links, r.normed_two, r.side_three, r.home_three, r.far_three)
    r.small_grads[...] = jnp.zeros_like(r.small_grads)

    @pl.loop(0, 4)
    def feed(at):
        @pl.when(at == 1)
        def from_sibling():
            for chunk in range(CHUNKS):
                spread_two.hand_over(chunk)
            spread_two.await_sibling()

        @pl.when(at == 3)
        def from_corner():
            spread_two.await_corner()

        rows = rows_at((me ^ at) * block, block)
        fc1 = flat_weight(r.full_b, r.wide)
        hidden = dot_nn(r.normed_two[rows, :], fc1) + r.vecs[6:7, :]
        below = 0.5 + 0.5 * lax.erf(hidden * 0.7071067811865476)
        density = 0.3989422804014327 * jnp.exp(-0.5 * hidden * hidden)
        low = (hidden * below).astype(BF)
        r.active[rows, :] = low
        fc2_t = flat_weight(r.full_c, r.wide)
        grad_active = dot_nn(r.given_all[rows, :], fc2_t)
        back = (grad_active * (below + hidden * density)).astype(BF)
        r.grad_hidden[rows, :] = back
        r.part_two[rows, :] = dot_nt(back, flat_weight(r.full_b, r.wide)).astype(BF)
        r.small_grads[6:7, :] += column_sum(back.astype(F32))

    sum_two.begin_side()
    sum_two.begin_home()
    for chunk in range(CHUNKS):
        sum_two.pass_on(chunk)
    scatter_b = GradScatter(links, r.grads_b, r.beside_b, r.landed_b, r.out_b)
    scatter_c = GradScatter(links, r.grads_c, r.beside_c, r.landed_c, r.out_c)

    @pl.loop(0, width // block)
    def weigh(at):
        columns = rows_at(at * block, block)
        split_rows(
            dot_tn(r.normed_two[:, columns], r.grad_hidden[...]), r.grads_b, at * block, r.wide
        )
        split_rows(dot_tn(r.given_all[:, columns], r.active[...]), r.grads_c, at * block, r.wide)

    scatter_b.begin()
    scatter_c.begin()
    links.sent(spread_two.corner_in)

    @pl.loop(0, 4)
    def branch(at):
        rows = rows_at(at * block, block)
        made = dot_nt(r.active[rows, :], flat_weight(r.full_c, r.wide))
        r.normed_two[rows, :] = made.astype(BF)

    spread_three = RowSpread(links, r.attended_own, r.rows_all)
    for chunk in range(CHUNKS):
        cut = sum_two.cut(chunk)
        grad = sum_two.total(chunk)
        back, unit = layer_norm_back(r.middle[cut, :], grad, vec(gain_two))
        given = r.cotangent[cut, :].astype(F32)
        row = given + back
        r.grad_middle[cut, :] = row
        low = row.astype(BF)
        r.attended_own[cut, :] = low
        spread_three.give(chunk)
        r.small_grads[gain_two : gain_two + 1, :] += column_sum(grad * unit)
        r.small_grads[shift_two : shift_two + 1, :] += column_sum(grad)
        r.small_grads[bias_out : bias_out + 1, :] += column_sum(low.astype(F32))
        r.small_grads[bias_fc2 : bias_fc2 + 1, :] += column_sum(given)
    sum_three.begin_side()
    sum_three.begin_home()
    for step in range(1, links.num_far):
        scatter_b.pass_on(step)
    for chunk in range(CHUNKS):
        spread_three.hand_over(chunk)
    for chunk in range(CHUNKS):
        sum_three.pass_on(chunk)
    spread_three.await_sibling()
    spread_three.await_corner()

    @pl.loop(0, num_blocks)
    def prepare(at):
        rows = rows_at(at * BLOCK, BLOCK)
        low = dot_nn(r.rows_all[rows, :], flat_weight(r.full_a, r.wide)[:, qkv:]).astype(BF)
        r.grad_mixed[rows, :] = low
        r.turned[:, rows] = jnp.transpose(r.keys[rows, :])
        both = jnp.transpose(low.astype(F32) * r.mixed[rows, :].astype(F32))
        for head in range(heads):
            r.inner[at, head : head + 1, :] = column_sum(both[head * HD : (head + 1) * HD, :])

    for step in range(1, links.num_far):
        scatter_c.pass_on(step)
    r.grad_keys[...] = jnp.zeros_like(r.grad_keys)
    r.grad_values[...] = jnp.zeros_like(r.grad_values)

    @pl.loop(0, num_blocks)
    def attend_back(at):
        rows = rows_at(at * BLOCK, BLOCK)
        asked, given = r.query[rows, :], r.grad_mixed[rows, :]
        keys_ids = jnp.concatenate([r.seg_wide[...]] * (BLOCK // 128), axis=1)
        query_ids = r.seg_row[0:1, rows].astype(F32)
        r.mask[...] = jnp.where(keys_ids == query_ids, 0.0, -1e30)
        asked_heads = [head_part(asked, head) for head in range(heads)]
        given_heads = [head_part(given, head) for head in range(heads)]
        made = []
        for head in range(heads):
            lanes = slice(head * BLOCK, (head + 1) * BLOCK)
            scores = dot_nt(r.keys[...], asked_heads[head]) + r.mask[...]
            probs = jnp.exp(scores - r.stats[at, head : head + 1, :])
            slopes = dot_nt(r.values[...], given_heads[head]) - r.inner[at, head : head + 1, :]
            slopes = (probs * slopes).astype(BF)
            r.active[:, lanes] = probs.astype(BF)
            r.grad_hidden[:, lanes] = slopes
            made.append(dot_nn(r.turned[head * HD : (head + 1) * HD, :], slopes))
        r.grad_values[...] += dot_nn(r.active[...], jnp.concatenate(given_heads, axis=0))
        r.grad_keys[...] += dot_nn(r.grad_hidden[...], jnp.concatenate(asked_heads, axis=0))
        turned = jnp.transpose(jnp.concatenate(made, axis=0)) * 0.125
        r.grad_proj[rows, :heads_width] = turned.astype(BF)

    links.sent(sum_one.side_in + sum_one.home_in)
    sum_four = RowSum(links, r.part_one, r.side_one, r.home_one, r.far_one)

    @pl.loop(0, num_blocks)
    def project_back(at):
        spot = lax.rem(at + (1 - upper) * (num_blocks // 2), num_blocks)
        rows = rows_at(spot * BLOCK, BLOCK)
        low_keys = r.grad_keys[rows, :].astype(BF)
        low_values = r.grad_values[rows, :].astype(BF)
        low_query = r.grad_proj[rows, :heads_width]
        whole = jnp.concatenate([low_query, low_keys, low_values], axis=1)
        r.grad_proj[rows, :] = whole
        made = dot_nt(whole, flat_weight(r.full_a, r.wide)[:, :qkv])
        r.part_one[rows, :] = made.astype(BF)
        wide_sum = column_sum(whole.astype(F32))
        r.small_grads[7:8, 0:heads_width] += wide_sum[:, 0:heads_width]
        r.small_grads[7:8, LANE_GAP : LANE_GAP + heads_width] += wide_sum[:, 2 * heads_width :]

        @pl.when(at == num_blocks // 2 - 1)
        def send_side():
            sum_four.begin_side()

    sum_four.begin_home()
    for chunk in range(CHUNKS):
        sum_four.pass_on(chunk)

    scatter_a = GradScatter(links, r.grads_a, r.beside_a, r.landed_a, r.out_a)

    @pl.loop(0, width // block)
    def weigh_in(at):
        columns = rows_at(at * block, block)
        both = jnp.concatenate(
            [
                dot_tn(r.normed[:, columns], r.grad_proj[...]),
                dot_tn(r.rows_all[:, columns], r.mixed[...]),
            ],
            axis=1,
        )
        split_rows(both, r.grads_a, at * block, r.wide)

    scatter_a.begin()
    for chunk in range(CHUNKS):
        cut = sum_three.cut(chunk)
        row = r.middle[cut, :] + (sum_three.total(chunk) + vec(bias_fc2))
        r.output[cut, :] = row.astype(BF)
    for step in range(1, links.num_far):
        scatter_a.pass_on(step)
    scatter_b.end()
    scatter_c.end()

    for chunk in range(CHUNKS):
        cut = sum_four.cut(chunk)
        grad = sum_four.total(chunk)
        back, unit = layer_norm_back(r.frames[cut, :].astype(F32), grad, vec(gain_one))
        r.grad_frames[cut, :] = r.grad_middle[cut, :] + back
        r.small_grads[gain_one : gain_one + 1, :] += column_sum(grad * unit)
        r.small_grads[shift_one : shift_one + 1, :] += column_sum(grad)

    back_group = [
        links.copy(r.small_grads, r.small_group_back.at[at], device)
        for at, device in enumerate((links.sibling, links.across, links.corner))
    ]
    back_dp = [
        links.copy(r.small_total, r.small_dp.at[at], other)
        for at, other in enumerate(links.others)
    ]
    for made in back_group:
        made.start()
    total = r.small_grads[...]
    for at, made in enumerate(back_group):
        made.wait_recv()
        total = total + jnp.where(
            lax.broadcasted_iota(jnp.int32, total.shape, 0) < 6, r.small_group_back[at], 0.0
        )
    r.small_total[...] = total
    for made in back_dp:
        made.start()
    scatter_a.end()
    for at, made in enumerate(back_dp):
        made.wait_recv()
        total = total + r.small_dp[at]
    own = (dp * 4 + me) * (width // (4 * num_dp))
    r.small_out[0:6, :] = pltpu.roll(total[0:6, :], lax.rem(width - own, width), 1)
    own = dp * (HD // num_dp)
    r.small_out[6:8, :] = pltpu.roll(total[6:8, :], lax.rem(width - own, width), 1)
    links.finish()


def copy_count(num_dp):
    far = num_dp // 2
    smalls = 2 * (num_dp - 1 + 3)
    spreads = 4 * 3 * CHUNKS
    weights = 3 * 2 * (2 * far - 1)
    sums = 4 * 3 * CHUNKS
    scatters = 3 * (2 * far - 1)
    return smalls + spreads + weights + sums + scatters


def layer(num_dp, seg, frames, cotangent, small, shard_a, shard_b, shard_c):
    block, width = frames.shape
    length, slab = 4 * block, shard_a.shape[0]
    heads_width = width // 4
    num_blocks = length // BLOCK
    vmem, hbm = pl.BlockSpec(memory_space=pltpu.VMEM), pl.BlockSpec(memory_space=pl.ANY)
    inputs = [
        ("seg_row", seg, vmem),
        ("frames", frames, vmem),
        ("cotangent", cotangent, vmem),
        ("small", small, vmem),
        ("shard_a", shard_a, vmem),
        ("shard_b", shard_b, vmem),
        ("shard_c", shard_c, vmem),
    ]
    outputs = [
        ("output", (block, width), BF),
        ("grad_frames", (block, width), F32),
        ("out_a", (slab, width), F32),
        ("out_b", (slab, width), F32),
        ("out_c", (slab, width), F32),
        ("small_out", (8, width), F32),
    ]
    scratch = [("rows_all", (length, width), BF), ("given_all", (length, width), BF)]
    scratch += [("normed", (length, width), BF), ("normed_two", (length, width), BF)]
    scratch += [("active", (length, width), BF), ("grad_hidden", (length, width), BF)]
    scratch += [(f"full_{tag}", (num_dp, slab, width), BF) for tag in "abc"]
    scratch += [(f"grads_{tag}", (num_dp, slab, width), BF) for tag in "abc"]
    for tag in "abc":
        scratch += [
            (f"{kind}_{tag}", (num_dp // 2, slab, width), BF)
            for kind in ("beside", "landed")
        ]
    for tag in ("one", "two", "three"):
        if tag != "three":
            scratch += [(f"part_{tag}", (length, width), BF)]
        scratch += [
            (f"{kind}_{tag}", (block, width), BF) for kind in ("side", "home", "far")
        ]
    scratch += [
        (name, (length, heads_width), BF)
        for name in ("query", "keys", "values", "mixed", "grad_mixed")
    ]
    scratch += [
        ("turned", (heads_width, length), BF),
        ("grad_keys", (length, heads_width), F32),
        ("grad_values", (length, heads_width), F32),
        ("grad_proj", (length, 3 * heads_width), BF),
        ("mask", (length, BLOCK), F32),
        ("seg_wide", (length, 128), F32),
        ("stats", (num_blocks, 8, BLOCK), F32),
        ("inner", (num_blocks, 8, BLOCK), F32),
        ("middle", (block, width), F32),
        ("grad_middle", (block, width), F32),
        ("normed_own", (block, width), BF),
        ("attended_own", (block, width), BF),
        ("vecs", (8, width), F32),
        ("wide", (width if slab % 16 else 8, width), F32),
    ]
    for name in ("small_mine", "small_sum", "small_grads", "small_total"):
        scratch += [(name, (8, width), F32)]
    for name in ("small_group", "small_group_back"):
        scratch += [(name, (3, 8, width), F32)]
    scratch += [("small_dp", (num_dp - 1, 8, width), F32)]
    count = copy_count(num_dp)
    names = [name for name, _, _ in inputs + outputs + scratch] + ["send_sems", "recv_sems"]
    return pl.pallas_call(
        functools.partial(layer_kernel, num_dp, names),
        out_shape=[jax.ShapeDtypeStruct(shape, kind) for _, shape, kind in outputs],
        in_specs=[spec for _, _, spec in inputs],
        out_specs=[vmem] * len(outputs),
        scratch_shapes=[pltpu.VMEM(shape, kind) for _, shape, kind in scratch]
        + [pltpu.SemaphoreType.DMA((count,))] * 2,
        compiler_params=pltpu.CompilerParams(
            collective_id=0, has_side_effects=True, vmem_limit_bytes=VMEM_BYTES
        ),
        name="layer",
    )(*[value for _, value, _ in inputs])


def on_device(
    num_dp,
    frames,
    segments,
    norm1_gain,
    norm1_shift,
    in_weight,
    proj_bias,
    out_weight,
    out_bias,
    norm2_gain,
    norm2_shift,
    fc1_weight,
    fc1_bias,
    fc2_weight,
    fc2_bias,
    cotangent,
):
    width = frames.shape[1]
    slab, _, heads_width = in_weight.shape
    heads = heads_width // HD
    own = norm1_gain.shape[0]
    share = HD // num_dp
    vecs = jnp.stack([norm1_gain, norm1_shift, norm2_gain, norm2_shift, out_bias, fc2_bias])
    vecs = jnp.pad(vecs, ((0, 0), (0, width - own)))
    fc1_row = jnp.pad(fc1_bias.astype(F32), ((0, 0), (0, HD - share))).reshape(1, width)
    proj_row = jnp.pad(
        proj_bias.astype(F32),
        ((0, 0), (0, LANE_GAP // HD - heads), (0, HD - share)),
    ).reshape(1, 2 * LANE_GAP)
    proj_row = jnp.pad(proj_row, ((0, 0), (0, width - 2 * LANE_GAP)))
    small = jnp.concatenate([vecs, fc1_row, proj_row], axis=0)
    shard_a = jnp.concatenate([in_weight.reshape(slab, 3 * heads_width), out_weight.T], axis=1)
    output, grad_frames, g_a, g_b, g_c, sums = layer(
        num_dp, segments, frames, cotangent, small, shard_a, fc1_weight, fc2_weight.T
    )
    g_in = g_a[:, : 3 * heads_width].reshape(slab, 3, heads_width)
    g_out = g_a[:, 3 * heads_width :].T
    mine = sums[0:6, :own]
    g_fc1b = sums[6].reshape(-1, HD)[:, :share]
    g_proj = sums[7, : 2 * LANE_GAP].reshape(2, LANE_GAP // HD, HD)[:, :heads, :share]
    return (
        output,
        grad_frames,
        mine[0],
        mine[1],
        g_in,
        g_proj,
        g_out,
        mine[4],
        mine[2],
        mine[3],
        g_b,
        g_fc1b,
        g_c.T,
        mine[5],
    )


def solution(mesh):
    in_specs = (
        P(("dp", "tensor"), None),
        P("dp", None),
        P(("dp", "tensor")),
        P(("dp", "tensor")),
        P("dp", None, "tensor"),
        P(None, "tensor", "dp"),
        P("tensor", "dp"),
        P(("dp", "tensor")),
        P(("dp", "tensor")),
        P(("dp", "tensor")),
        P("dp", "tensor"),
        P("tensor", "dp"),
        P("tensor", "dp"),
        P(("dp", "tensor")),
        P(("dp", "tensor"), None),
    )
    out_specs = (
        P(("dp", "tensor"), None),
        P(("dp", "tensor"), None),
        P(("dp", "tensor")),
        P(("dp", "tensor")),
        P("dp", None, "tensor"),
        P(None, "tensor", "dp"),
        P("tensor", "dp"),
        P(("dp", "tensor")),
        P(("dp", "tensor")),
        P(("dp", "tensor")),
        P("dp", "tensor"),
        P("tensor", "dp"),
        P("tensor", "dp"),
        P(("dp", "tensor")),
    )
    return jax.shard_map(
        functools.partial(on_device, mesh.shape["dp"]),
        mesh=mesh,
        in_specs=in_specs,
        out_specs=out_specs,
        check_vma=False,
    )
```

time: 856 us -> 200 us (0.23); the launches traced: 846 us -> 200 us
  waiting for transfers between devices: 323 us -> 0 us
  blocking collectives: 239 us -> 0 us
  Pallas kernels: 0 us -> 182 us
  matrix products: 135 us -> 0 us
  other arithmetic: 77.1 us -> 1.4 us
  local copies, waits for them, and re-layouts: 43.5 us -> 15.9 us
  between operations: 17.1 us -> 0.72 us
  loops' own time: 10.2 us -> 0 us
    reduce_scatter x7 -> x0, waiting for transfers between devices: 239 us -> none  [the longest x1 72.9 us: on_device(): lax.psum_scatter(grad_fc1, 'dp', scatter_dimension=0, tiled=True)]
    pallas_call x0 -> x1, Pallas kernels: none -> 182 us  [layer(): pl.pallas_call(functools.partial(layer_kernel, num_dp, names), out_shape=...]
    dot_general x32 -> x0, matrix products: 131 us -> none  [the longest x28 115 us: contract(): return jnp.einsum(pattern, left, right, preferred_element_type=jnp.float32)]
    all_gather x4 -> x0, blocking collectives: 121 us -> none  [the longest x1 33.8 us: on_device(): lax.all_gather(in_weight, 'dp', axis=0, tiled=True)]
    unnamed x3 -> x0, blocking collectives: 117 us -> none
    all_gather x6 -> x0, waiting for transfers between devices: 82.1 us -> none  [the longest x1 33.9 us: on_device(): lax.all_gather(fc2_weight, 'dp', axis=1, tiled=True)]
    convert_element_type x8 -> x0, other arithmetic: 38.2 us -> none  [the longest x3 28.3 us: backward_block(): grad_scores = (attn_probs * (grad_probs - row_inner)).astype(jnp.bfloat16)]
    reduce_sum x13 -> x0, other arithmetic: 24.2 us -> none  [the longest x3 8.39 us: forward_block(): row_total = jnp.sum(exp_scores, axis=-1, keepdims=True)]
  transfers between devices with their start and end apart: 14 -> 0, of which waited for: 8 -> 0; matrix products, arithmetic and copies ran while one was open for 20% -> 0% of each run, Pallas kernels for 0% -> 0%
where the time goes in v1:
time: 200 us
  Pallas kernels  182 us (91%)
  local copies, waits for them, and re-layouts  15.9 us (8%)
    pallas_call x1, Pallas kernels, layer(): pl.pallas_call(functools.partial(layer_kernel, num_dp, names), out_shape=...  182 us
    unnamed x20, local copies, waits for them, and re-layouts  9.65 us

profile of v1, /device:TPU:0, one launch (start us, length us, event | category | flops | bytes accessed | tf_op | source)
XLA Modules:
  0.0 199.7 jit_solution(6288214782739699892)
XLA Ops:
  0.6 0.8 stack.27
  1.4 0.7 copy.59
  2.1 0.1 reshape.46
  2.2 0.8 copy.47
  3.0 0.1 reshape.50
  3.0 0.6 fusion.refs_3_
  3.7 0.9 copy.50
  4.6 1.1 copy.49
  5.6 0.2 copy.51
  5.8 0.8 pad_maximum_fusion.refs_4_
  6.5 181.7 %layer.1 = (bf16[384,768]{1,0:T(8,128)(2,1)}, f32[384,768]{1,0:T(8,128)}, f32[96,768]{1,0:T(8,128)}, f32[96,768]{1,0:T(8,128)}, f32[96,768]{1,0:T(8,128)}, /*index=5*/f32[8,768]{1,0:T(8,128)}) custom-call(s32[1,1536]{1,0:T(1,128)} %refs_0_.1, bf16[384,768]{1,0:T(8,128)(2,1)} %refs_1_.1, bf16[384,768]{1,0:T(8,128)(2,1)} %refs_2_.1, f32[8,768]{1,0:T(8,128)} %fusion.refs_3_, ...), custom_call_target="tpu_custom_call" | custom-call | tf_op jit(solution)/shard_map/layer/pallas_call | solution.py:744
  188.3 0.0 copy-start.1
  188.3 1.4 slice_bitcast_fusion.1
  189.7 1.0 slice.45
  190.7 0.1 copy.52
  190.9 0.0 copy-start
  190.9 0.9 copy.55
  191.7 0.7 slice_reduce_fusion.1
  192.5 0.1 reshape_squeeze.6
  192.6 0.6 copy.57
  193.1 1.0 slice_bitcast_fusion
  194.1 0.7 copy.56
  194.9 0.8 slice_reduce_fusion
  195.6 0.1 reshape_squeeze.7
  195.7 0.7 copy.58
  196.4 0.0 copy-done.1
  196.4 0.8 copy.64
  197.2 0.0 copy-done
  197.2 0.0 copy-start.3
  197.2 0.0 copy-start.2
  197.2 1.0 copy.65
  198.2 0.1 copy-done.3
  198.3 0.7 copy.66
  199.0 0.0 copy-done.2
  199.0 0.7 copy.67
  (3 shorter events, 0.0 us)
Async XLA Ops:
  188.3 8.1 %copy-start.1 = (bf16[384,768]{1,0:T(8,128)(2,1)S(1)}, bf16[384,768]{1,0:T(8,128)(2,1)}, u32[]{:S(2)}) copy-start(bf16[384,768]{1,0:T(8,128)(2,1)} %get-tuple-element.88) | copy-start | bytes 1769476
  190.9 6.3 %copy-start = (f32[384,768]{1,0:T(8,128)S(1)}, f32[384,768]{1,0:T(8,128)}, u32[]{:S(2)}) copy-start(f32[384,768]{1,0:T(8,128)} %get-tuple-element.89) | copy-start | bytes 3538948
  197.2 1.1 copy-start.3
  197.2 1.8 copy-start.2

commit v2 on v1

--- a/solution.py
+++ b/solution.py
@@ -139,9 +139,11 @@
     def begin(self):
         for made in self.first.values():
             made.start()
+        self.full[self.links.dp] = self.shard[...]
+
+    def begin_beside(self):
         for half in range(self.halves):
             self.second[half, 0].start()
-        self.full[self.links.dp] = self.shard[...]
 
     def forward(self, half):
         for step in range(1, self.links.num_far):
@@ -319,7 +321,6 @@
     heads = heads_width // HD
     qkv = 3 * heads_width
     upper = me // 2
-    parts = 2 * CHUNKS
 
     links.greet(links.others + [links.sibling, links.across, links.corner])
 
@@ -344,6 +345,7 @@
     for chunk in range(CHUNKS):
         frame_rows.give(chunk)
     spread_a.begin()
+    spread_a.begin_beside()
     for chunk in range(CHUNKS):
         given_rows.give(chunk)
     spread_b.begin()
@@ -370,18 +372,25 @@
     def vec(at):
         return r.vecs[at : at + 1, :]
 
-    for chunk in range(CHUNKS):
-        frame_rows.hand_over(chunk)
     spread_a.forward(0)
+    frame_rows.hand_over(0)
     spread_a.forward(1)
+    spread_b.begin_beside()
+    spread_c.begin_beside()
+    frame_rows.hand_over(1)
     frame_rows.await_sibling()
-    frame_rows.await_corner()
     spread_a.end()
-    links.sent(frame_rows.corner_in)
 
     @pl.loop(0, num_blocks)
     def project(at):
-        rows = rows_at(at * BLOCK, BLOCK)
+        spot = lax.rem(at + upper * (num_blocks // 2), num_blocks)
+        rows = rows_at(spot * BLOCK, BLOCK)
+
+        @pl.when(at == num_blocks // 2)
+        def from_across():
+            frame_rows.hand_over(2)
+            frame_rows.await_corner()
+
         low = layer_norm(
             r.rows_all[rows, :].astype(F32), vec(gain_one), vec(shift_one)
         ).astype(BF)
@@ -419,39 +428,66 @@
         r.mixed[rows, :] = out
         r.part_one[rows, :] = dot_nt(out, flat_weight(r.full_a, r.wide)[:, qkv:]).astype(BF)
 
-        @pl.when(at == 0)
-        def early():
+        def after(step, core=None):
+            return pl.when((at == step) if core is None else ((at == step) & (me % 2 == core)))
+
+        @after(0, 1)
+        def upper_first():
+            sum_one.side_in[0].start()
+            sum_one.side_in[1].start()
+
+        @after(0)
+        def weights_first():
+            spread_b.forward(0)
+
+        @after(1, 0)
+        def lower_second():
+            sum_one.pass_on(0)
+            sum_one.pass_on(1)
+            sum_one.side_in[0].start()
+
+        @after(1, 1)
+        def upper_second():
+            sum_one.side_in[2].start()
+
+        @after(1)
+        def rows_first():
             given_rows.hand_over(0)
-            spread_b.forward(0)
-
-        @pl.when(at == 1)
-        def second():
+
+        @after(2, 0)
+        def lower_third():
+            sum_one.side_in[1].start()
+            sum_one.side_in[2].start()
+            sum_one.pass_on(2)
+
+        @after(2, 1)
+        def upper_third():
+            sum_one.pass_on(0)
+
+        @after(3, 1)
+        def upper_fourth():
+            sum_one.pass_on(1)
+            sum_one.pass_on(2)
+
+        @after(3)
+        def rows_second():
             given_rows.hand_over(1)
-            given_rows.hand_over(2)
-
-        @pl.when(at == 2)
-        def third():
-            sum_one.begin_side()
+
+        @after(4)
+        def weights_second():
             spread_b.forward(1)
 
-        @pl.when(at == 3)
-        def fourth():
-            for chunk in range(CHUNKS):
-                sum_one.pass_on(chunk)
-
-        @pl.when(at == 4)
-        def fifth():
-            spread_c.forward(0)
-
     sum_one.begin_home()
-    spread_c.forward(1)
+    given_rows.hand_over(2)
     for chunk in range(CHUNKS):
         cut = sum_one.cut(chunk)
         row = r.frames[cut, :].astype(F32) + (sum_one.total(chunk) + vec(bias_out))
         r.middle[cut, :] = row
         r.normed_own[cut, :] = layer_norm(row, vec(gain_two), vec(shift_two)).astype(BF)
         spread_two.give(chunk)
-    links.sent(sum_one.far_in)
+        if chunk < 2:
+            spread_c.forward(chunk)
+    links.sent(sum_one.far_in + frame_rows.corner_in)
     given_rows.await_sibling()
     given_rows.await_corner()
     spread_b.end()
@@ -461,59 +497,64 @@
     sum_three = RowSum(links, r.normed_two, r.side_three, r.home_three, r.far_three)
     r.small_grads[...] = jnp.zeros_like(r.small_grads)
 
-    @pl.loop(0, 4)
+    @pl.loop(0, 2 * CHUNKS)
     def feed(at):
-        @pl.when(at == 1)
-        def from_sibling():
-            for chunk in range(CHUNKS):
+        def when_at(step):
+            return pl.when(at == step)
+
+        for chunk in range(CHUNKS):
+
+            @when_at(2 * chunk)
+            def near(chunk=chunk):
+                spread_two.sibling_in[chunk].wait_recv()
+
+            @when_at(2 * chunk + 1)
+            def remote(chunk=chunk):
                 spread_two.hand_over(chunk)
-            spread_two.await_sibling()
-
-        @pl.when(at == 3)
-        def from_corner():
-            spread_two.await_corner()
-
-        rows = rows_at((me ^ at) * block, block)
-        fc1 = flat_weight(r.full_b, r.wide)
-        hidden = dot_nn(r.normed_two[rows, :], fc1) + r.vecs[6:7, :]
+                if chunk:
+                    sum_two.pass_on(chunk - 1)
+                spread_two.corner_in[chunk].wait_recv()
+
+        chunk_start = (at // 2) * (block // CHUNKS)
+        member = me ^ (2 * (at % 2))
+        rows = rows_at(member * block + chunk_start, block // CHUNKS)
+        rows_too = rows_at((member ^ 1) * block + chunk_start, block // CHUNKS)
+
+        def both(ref):
+            return jnp.concatenate([ref[rows, :], ref[rows_too, :]], axis=0)
+
+        def put(ref, value):
+            low = value.astype(BF)
+            ref[rows, :] = low[: block // CHUNKS]
+            ref[rows_too, :] = low[block // CHUNKS :]
+
+        hidden = dot_nn(both(r.normed_two), flat_weight(r.full_b, r.wide)) + r.vecs[6:7, :]
         below = 0.5 + 0.5 * lax.erf(hidden * 0.7071067811865476)
         density = 0.3989422804014327 * jnp.exp(-0.5 * hidden * hidden)
-        low = (hidden * below).astype(BF)
-        r.active[rows, :] = low
-        fc2_t = flat_weight(r.full_c, r.wide)
-        grad_active = dot_nn(r.given_all[rows, :], fc2_t)
+        put(r.active, hidden * below)
+        grad_active = dot_nn(both(r.given_all), flat_weight(r.full_c, r.wide))
         back = (grad_active * (below + hidden * density)).astype(BF)
-        r.grad_hidden[rows, :] = back
-        r.part_two[rows, :] = dot_nt(back, flat_weight(r.full_b, r.wide)).astype(BF)
+        put(r.grad_hidden, back)
+        put(r.part_two, dot_nt(back, flat_weight(r.full_b, r.wide)))
         r.small_grads[6:7, :] += column_sum(back.astype(F32))
 
-    sum_two.begin_side()
-    sum_two.begin_home()
-    for chunk in range(CHUNKS):
-        sum_two.pass_on(chunk)
+        for chunk in range(CHUNKS):
+
+            @when_at(2 * chunk)
+            def near_done(chunk=chunk):
+                sum_two.home_in[chunk].start()
+
+            @when_at(2 * chunk + 1)
+            def remote_done(chunk=chunk):
+                sum_two.side_in[chunk].start()
+
+    sum_two.pass_on(CHUNKS - 1)
     scatter_b = GradScatter(links, r.grads_b, r.beside_b, r.landed_b, r.out_b)
     scatter_c = GradScatter(links, r.grads_c, r.beside_c, r.landed_c, r.out_c)
 
-    @pl.loop(0, width // block)
-    def weigh(at):
-        columns = rows_at(at * block, block)
-        split_rows(
-            dot_tn(r.normed_two[:, columns], r.grad_hidden[...]), r.grads_b, at * block, r.wide
-        )
-        split_rows(dot_tn(r.given_all[:, columns], r.active[...]), r.grads_c, at * block, r.wide)
-
-    scatter_b.begin()
-    scatter_c.begin()
-    links.sent(spread_two.corner_in)
-
-    @pl.loop(0, 4)
-    def branch(at):
-        rows = rows_at(at * block, block)
-        made = dot_nt(r.active[rows, :], flat_weight(r.full_c, r.wide))
-        r.normed_two[rows, :] = made.astype(BF)
-
     spread_three = RowSpread(links, r.attended_own, r.rows_all)
-    for chunk in range(CHUNKS):
+
+    def second_norm_back(chunk):
         cut = sum_two.cut(chunk)
         grad = sum_two.total(chunk)
         back, unit = layer_norm_back(r.middle[cut, :], grad, vec(gain_two))
@@ -527,36 +568,90 @@
         r.small_grads[shift_two : shift_two + 1, :] += column_sum(grad)
         r.small_grads[bias_out : bias_out + 1, :] += column_sum(low.astype(F32))
         r.small_grads[bias_fc2 : bias_fc2 + 1, :] += column_sum(given)
-    sum_three.begin_side()
-    sum_three.begin_home()
-    for step in range(1, links.num_far):
-        scatter_b.pass_on(step)
-    for chunk in range(CHUNKS):
-        spread_three.hand_over(chunk)
-    for chunk in range(CHUNKS):
-        sum_three.pass_on(chunk)
-    spread_three.await_sibling()
-    spread_three.await_corner()
-
-    @pl.loop(0, num_blocks)
-    def prepare(at):
-        rows = rows_at(at * BLOCK, BLOCK)
-        low = dot_nn(r.rows_all[rows, :], flat_weight(r.full_a, r.wide)[:, qkv:]).astype(BF)
-        r.grad_mixed[rows, :] = low
-        r.turned[:, rows] = jnp.transpose(r.keys[rows, :])
-        both = jnp.transpose(low.astype(F32) * r.mixed[rows, :].astype(F32))
-        for head in range(heads):
-            r.inner[at, head : head + 1, :] = column_sum(both[head * HD : (head + 1) * HD, :])
-
-    for step in range(1, links.num_far):
-        scatter_c.pass_on(step)
+
+    second_norm_back(0)
+
+    @pl.loop(0, width // block)
+    def weigh_one(at):
+        columns = rows_at(at * block, block)
+        made = dot_tn(r.normed_two[:, columns], r.grad_hidden[...])
+        split_rows(made, r.grads_b, at * block, r.wide)
+
+    scatter_b.begin()
+    second_norm_back(1)
+
+    @pl.loop(0, width // block)
+    def weigh_two(at):
+        columns = rows_at(at * block, block)
+        made = dot_tn(r.given_all[:, columns], r.active[...])
+        split_rows(made, r.grads_c, at * block, r.wide)
+
+    scatter_c.begin()
+    second_norm_back(2)
+    links.sent(spread_two.corner_in)
+
+    @pl.loop(0, 4)
+    def branch(at):
+        rows = rows_at((me ^ (3 - at)) * block, block)
+        made = dot_nt(r.active[rows, :], flat_weight(r.full_c, r.wide))
+        r.normed_two[rows, :] = made.astype(BF)
+
+        @pl.when(at == 0)
+        def corner_done():
+            sum_three.begin_side()
+
+        @pl.when(at == 2)
+        def sibling_done():
+            sum_three.begin_home()
+
     r.grad_keys[...] = jnp.zeros_like(r.grad_keys)
     r.grad_values[...] = jnp.zeros_like(r.grad_values)
 
     @pl.loop(0, num_blocks)
+    def turn_keys(at):
+        rows = rows_at(at * BLOCK, BLOCK)
+        r.turned[:, rows] = jnp.transpose(r.keys[rows, :])
+
+    spread_three.await_sibling()
+
+    @pl.loop(0, num_blocks)
     def attend_back(at):
-        rows = rows_at(at * BLOCK, BLOCK)
-        asked, given = r.query[rows, :], r.grad_mixed[rows, :]
+        def when_at(step):
+            return pl.when(at == step)
+
+        @when_at(1)
+        def first_service():
+            for chunk in range(CHUNKS):
+                sum_three.pass_on(chunk)
+            spread_three.hand_over(0)
+            scatter_b.pass_on(1)
+            scatter_b.pass_on(2)
+
+        @when_at(2)
+        def second_service():
+            spread_three.hand_over(1)
+            for step in range(3, links.num_far):
+                scatter_b.pass_on(step)
+
+        @when_at(3)
+        def third_service():
+            spread_three.hand_over(2)
+            spread_three.await_corner()
+
+        @when_at(4)
+        def fourth_service():
+            scatter_c.pass_on(1)
+
+        @when_at(5)
+        def fifth_service():
+            for step in range(2, links.num_far):
+                scatter_c.pass_on(step)
+
+        spot = lax.rem(at + upper * (num_blocks // 2), num_blocks)
+        rows = rows_at(spot * BLOCK, BLOCK)
+        asked = r.query[rows, :]
+        given = dot_nn(r.rows_all[rows, :], flat_weight(r.full_a, r.wide)[:, qkv:]).astype(BF)
+        joint = jnp.transpose(given.astype(F32) * r.mixed[rows, :].astype(F32))
         keys_ids = jnp.concatenate([r.seg_wide[...]] * (BLOCK // 128), axis=1)
         query_ids = r.seg_row[0:1, rows].astype(F32)
         r.mask[...] = jnp.where(keys_ids == query_ids, 0.0, -1e30)
@@ -566,8 +661,9 @@
         for head in range(heads):
             lanes = slice(head * BLOCK, (head + 1) * BLOCK)
             scores = dot_nt(r.keys[...], asked_heads[head]) + r.mask[...]
-            probs = jnp.exp(scores - r.stats[at, head : head + 1, :])
-            slopes = dot_nt(r.values[...], given_heads[head]) - r.inner[at, head : head + 1, :]
+            probs = jnp.exp(scores - r.stats[spot, head : head + 1, :])
+            inner = column_sum(joint[head * HD : (head + 1) * HD, :])
+            slopes = dot_nt(r.values[...], given_heads[head]) - inner
             slopes = (probs * slopes).astype(BF)
             r.active[:, lanes] = probs.astype(BF)
             r.grad_hidden[:, lanes] = slopes
@@ -580,10 +676,9 @@
     links.sent(sum_one.side_in + sum_one.home_in)
     sum_four = RowSum(links, r.part_one, r.side_one, r.home_one, r.far_one)
 
-    @pl.loop(0, num_blocks)
+    @pl.loop(0, 4)
     def project_back(at):
-        spot = lax.rem(at + (1 - upper) * (num_blocks // 2), num_blocks)
-        rows = rows_at(spot * BLOCK, BLOCK)
+        rows = rows_at((me ^ (3 - at)) * block, block)
         low_keys = r.grad_keys[rows, :].astype(BF)
         low_values = r.grad_values[rows, :].astype(BF)
         low_query = r.grad_proj[rows, :heads_width]
@@ -595,13 +690,18 @@
         r.small_grads[7:8, 0:heads_width] += wide_sum[:, 0:heads_width]
         r.small_grads[7:8, LANE_GAP : LANE_GAP + heads_width] += wide_sum[:, 2 * heads_width :]
 
-        @pl.when(at == num_blocks // 2 - 1)
-        def send_side():
+        @pl.when(at == 0)
+        def corner_done():
             sum_four.begin_side()
 
-    sum_four.begin_home()
-    for chunk in range(CHUNKS):
-        sum_four.pass_on(chunk)
+        @pl.when(at == 1)
+        def across_done():
+            for chunk in range(CHUNKS):
+                sum_four.pass_on(chunk)
+
+        @pl.when(at == 2)
+        def sibling_done():
+            sum_four.begin_home()
 
     scatter_a = GradScatter(links, r.grads_a, r.beside_a, r.landed_a, r.out_a)
 
@@ -716,7 +816,7 @@
         ]
     scratch += [
         (name, (length, heads_width), BF)
-        for name in ("query", "keys", "values", "mixed", "grad_mixed")
+        for name in ("query", "keys", "values", "mixed")
     ]
     scratch += [
         ("turned", (heads_width, length), BF),
@@ -726,7 +826,6 @@
         ("mask", (length, BLOCK), F32),
         ("seg_wide", (length, 128), F32),
         ("stats", (num_blocks, 8, BLOCK), F32),
-        ("inner", (num_blocks, 8, BLOCK), F32),
         ("middle", (block, width), F32),
         ("grad_middle", (block, width), F32),
         ("normed_own", (block, width), BF),

time: 200 us -> 185 us (0.925)
  Pallas kernels: 182 us -> 166 us
    pallas_call x1, Pallas kernels: 182 us -> 166 us  [layer(): pl.pallas_call(functools.partial(layer_kernel, num_dp, names), out_shape=...]
where the time goes in v2:
time: 185 us; the launch traced here: 184 us
  Pallas kernels  166 us (90%)
  local copies, waits for them, and re-layouts  15.9 us (9%)
    pallas_call x1, Pallas kernels, layer(): pl.pallas_call(functools.partial(layer_kernel, num_dp, names), out_shape=...  166 us
    unnamed x20, local copies, waits for them, and re-layouts  9.65 us

profile of v2, /device:TPU:0, one launch (start us, length us, event | category | flops | bytes accessed | tf_op | source)
XLA Modules:
  0.0 184.3 jit_solution(17815780345272179857)
XLA Ops:
  0.6 0.8 stack.27
  1.4 0.7 copy.59
  2.1 0.1 reshape.46
  2.2 0.8 copy.47
  3.0 0.1 reshape.50
  3.0 0.6 fusion.refs_3_
  3.7 0.9 copy.50
  4.6 1.1 copy.49
  5.6 0.2 copy.51
  5.8 0.8 pad_maximum_fusion.refs_4_
  6.5 166.3 %layer.1 = (bf16[384,768]{1,0:T(8,128)(2,1)}, f32[384,768]{1,0:T(8,128)}, f32[96,768]{1,0:T(8,128)}, f32[96,768]{1,0:T(8,128)}, f32[96,768]{1,0:T(8,128)}, /*index=5*/f32[8,768]{1,0:T(8,128)}) custom-call(s32[1,1536]{1,0:T(1,128)} %refs_0_.1, bf16[384,768]{1,0:T(8,128)(2,1)} %refs_1_.1, bf16[384,768]{1,0:T(8,128)(2,1)} %refs_2_.1, f32[8,768]{1,0:T(8,128)} %fusion.refs_3_, ...), custom_call_target="tpu_custom_call" | custom-call | tf_op jit(solution)/shard_map/layer/pallas_call | solution.py:843
  172.9 0.0 copy-start.1
  172.9 1.4 slice_bitcast_fusion.1
  174.3 1.0 slice.45
  175.3 0.1 copy.52
  175.4 0.0 copy-start
  175.4 0.9 copy.55
  176.3 0.7 slice_reduce_fusion.1
  177.0 0.1 reshape_squeeze.6
  177.1 0.6 copy.57
  177.7 1.0 slice_bitcast_fusion
  178.7 0.7 copy.56
  179.4 0.8 slice_reduce_fusion
  180.2 0.1 reshape_squeeze.7
  180.3 0.7 copy.58
  180.9 0.0 copy-done.1
  180.9 0.8 copy.64
  181.7 0.0 copy-done
  181.7 0.0 copy-start.3
  181.7 0.0 copy-start.2
  181.7 1.0 copy.65
  182.8 0.1 copy-done.3
  182.9 0.7 copy.66
  183.6 0.0 copy-done.2
  183.6 0.7 copy.67
  (3 shorter events, 0.0 us)
Async XLA Ops:
  172.9 8.1 %copy-start.1 = (bf16[384,768]{1,0:T(8,128)(2,1)S(1)}, bf16[384,768]{1,0:T(8,128)(2,1)}, u32[]{:S(2)}) copy-start(bf16[384,768]{1,0:T(8,128)(2,1)} %get-tuple-element.88) | copy-start | bytes 1769476
  175.4 6.3 %copy-start = (f32[384,768]{1,0:T(8,128)S(1)}, f32[384,768]{1,0:T(8,128)}, u32[]{:S(2)}) copy-start(f32[384,768]{1,0:T(8,128)} %get-tuple-element.89) | copy-start | bytes 3538948
  181.7 1.1 copy-start.3
  181.7 1.8 copy-start.2

commit v3 on v2

--- a/solution.py
+++ b/solution.py
@@ -49,6 +49,17 @@
     return lax.dot_general(left, right, (((0,), (0,)), ((), ())), preferred_element_type=F32)
 
 
+def normal_parts(hidden):
+    bell = jnp.exp(-0.5 * hidden * hidden)
+    near = 1.0 / (1.0 + 0.23164189 * jnp.abs(hidden))
+    tail = near * (
+        0.127414796
+        + near * (-0.142248368 + near * (0.7107068705 + near * (-0.7265760135 + near * 0.5307027145)))
+    )
+    above = tail * bell
+    return jnp.where(hidden < 0.0, above, 1.0 - above), 0.3989422804014327 * bell
+
+
 def column_sum(block):
     return jnp.sum(block, axis=0, keepdims=True)
 
@@ -99,7 +110,7 @@
             pl.semaphore_signal(
                 barrier, inc=1, device_id=device, device_id_type=pl.DeviceIdType.MESH
             )
-        pl.semaphore_wait(barrier, len(devices))
+        return lambda: pl.semaphore_wait(barrier, len(devices))
 
     def sent(self, copies):
         for made in copies:
@@ -113,18 +124,17 @@
 
 
 class WeightSpread:
-    def __init__(self, links, shard, full, halves):
-        self.links, self.shard, self.full, self.halves = links, shard, full, halves
-        columns = shard.shape[-1] // halves
+    def __init__(self, links, shard, full, edges):
+        self.links, self.shard, self.full = links, shard, full
 
         def part(ref, half):
-            return ref.at[:, pl.ds(half * columns, columns)]
+            return ref.at[:, pl.ds(edges[half], edges[half + 1] - edges[half])]
 
         def place(origin, half):
-            return full.at[origin, :, pl.ds(half * columns, columns)]
+            return full.at[origin, :, pl.ds(edges[half], edges[half + 1] - edges[half])]
 
         self.first, self.second = {}, {}
-        for half in range(halves):
+        for half in range(len(edges) - 1):
             for step in range(1, links.num_far):
                 self.first[half, step] = links.copy(
                     part(shard, half), place(links.dp, half), (links.far(step), links.tensor)
@@ -136,23 +146,25 @@
                 spot = place(links.far_from(step), half)
                 self.second[half, step] = links.copy(spot, spot, links.beside)
 
-    def begin(self):
-        for made in self.first.values():
-            made.start()
+    def begin(self, half):
+        for step in range(1, self.links.num_far):
+            self.first[half, step].start()
+
+    def begin_beside(self, half):
+        self.second[half, 0].start()
+
+    def keep_own(self):
         self.full[self.links.dp] = self.shard[...]
-
-    def begin_beside(self):
-        for half in range(self.halves):
-            self.second[half, 0].start()
 
     def forward(self, half):
         for step in range(1, self.links.num_far):
             self.first[half, step].wait_recv()
             self.second[half, step].start()
 
-    def end(self):
-        for made in self.second.values():
-            made.wait_recv()
+    def end(self, halves):
+        for half in halves:
+            for step in range(self.links.num_far):
+                self.second[half, step].wait_recv()
 
 
 class RowSum:
@@ -288,13 +300,14 @@
             setattr(self, name, ref)
 
 
-def flat_weight(full, wide):
+def flat_weight(full, wide, start=0, stop=None):
     count, slab, width = full.shape
+    stop = stop or width
     if slab % 16 == 0:
-        return full[...].reshape(count * slab, width)
+        return full[:, :, start:stop].reshape(count * slab, stop - start)
     for at in range(count):
-        wide[at * slab : (at + 1) * slab, :] = full[at].astype(F32)
-    return wide[...].astype(BF)
+        wide[at * slab : (at + 1) * slab, start:stop] = full[at, :, start:stop].astype(F32)
+    return wide[:, start:stop].astype(BF)
 
 
 def split_rows(value, grads, start, wide):
@@ -310,6 +323,14 @@
         grads[start // slab + at] = wide[at * slab : (at + 1) * slab, :].astype(BF)
 
 
+def turn(value):
+    rows, columns = value.shape
+    tall = jnp.concatenate(
+        [value.astype(F32), jnp.zeros((rows, 128 - columns), F32)], axis=1
+    )
+    return jnp.transpose(tall)[:columns, :].astype(value.dtype)
+
+
 def layer_kernel(num_dp, names, *refs):
     r = Refs(names, refs)
     links = Links(num_dp, r.send_sems, r.recv_sems)
@@ -322,80 +343,113 @@
     qkv = 3 * heads_width
     upper = me // 2
 
-    links.greet(links.others + [links.sibling, links.across, links.corner])
-
+    await_all = links.greet(links.others + [links.sibling, links.across, links.corner])
+
+    small_group = [
+        links.copy(r.small_mine, r.small_group.at[at], device)
+        for at, device in enumerate((links.sibling, links.across, links.corner))
+    ]
     small_dp = [
-        links.copy(r.small_mine, r.small_dp.at[at], other) for at, other in enumerate(links.others)
-    ]
-    small_group = [
-        links.copy(r.small_sum, r.small_group.at[at], device)
-        for at, device in enumerate((links.sibling, links.across, links.corner))
+        links.copy(r.small_sum, r.small_dp.at[at], other) for at, other in enumerate(links.others)
     ]
     frame_rows = RowSpread(links, r.frames, r.rows_all)
     given_rows = RowSpread(links, r.cotangent, r.given_all)
-    spread_a = WeightSpread(links, r.shard_a, r.full_a, 2)
-    spread_b = WeightSpread(links, r.shard_b, r.full_b, 2)
-    spread_c = WeightSpread(links, r.shard_c, r.full_c, 2)
-
-    placed = pltpu.roll(r.small[0:6, :], (dp * 4 + me) * (width // (4 * num_dp)), 1)
-    r.small_mine[0:6, :] = placed
-    r.small_mine[6:8, :] = pltpu.roll(r.small[6:8, :], dp * (HD // num_dp), 1)
-    for made in small_dp:
+    spread_a = WeightSpread(links, r.shard_a, r.full_a, (0, width // 2, width * 5 // 6, width))
+    spread_b = WeightSpread(links, r.shard_b, r.full_b, (0, width // 2, width))
+    spread_c = WeightSpread(links, r.shard_c, r.full_c, (0, width // 2, width))
+
+    r.shard_a[:, :qkv] = jnp.concatenate([r.in_weight[at] for at in range(3)], axis=1)
+    r.shard_a[:, qkv:] = turn(r.out_weight[...])
+    own, share = width // (4 * num_dp), HD // num_dp
+    r.small_mine[...] = jnp.zeros_like(r.small_mine)
+    for at in range(6):
+        r.small_mine[at : at + 1, 0:own] = getattr(r, f"vec_{at}")[...]
+    r.small_mine[0:6, :] = pltpu.roll(r.small_mine[0:6, :], (dp * 4 + me) * own, 1)
+    lane = lax.broadcasted_iota(jnp.int32, (1, width), 1)
+
+    def one_hot(rows, target):
+        return jnp.where(
+            lax.broadcasted_iota(jnp.int32, (rows, width), 0) == target, 1.0, 0.0
+        ).astype(BF)
+
+    tall = dot_nn(r.fc1_bias[...], one_hot(width // HD, lane // HD))
+    within = lane % HD - dp * share
+    r.small_mine[6:7, :] = column_sum(
+        jnp.where(lax.broadcasted_iota(jnp.int32, tall.shape, 0) == within, tall, 0.0)
+    )
+    row = jnp.zeros((1, width), F32)
+    for head in range(heads):
+        pair = dot_nn(r.proj_bias[head], one_hot(share, within))
+        for at in range(2):
+            here = lane // HD == at * (LANE_GAP // HD) + head
+            row = row + jnp.where(here, pair[at : at + 1, :], 0.0)
+    r.small_mine[7:8, :] = row
+    ids = r.seg_row[0:1, :].astype(F32)
+    r.seg_wide[...] = jnp.transpose(jnp.broadcast_to(ids, (128, length)))
+    await_all()
+    for made in small_group:
         made.start()
     for chunk in range(CHUNKS):
         frame_rows.give(chunk)
-    spread_a.begin()
-    spread_a.begin_beside()
-    for chunk in range(CHUNKS):
-        given_rows.give(chunk)
-    spread_b.begin()
-    spread_c.begin()
-
-    ids = r.seg_row[0:1, :].astype(F32)
-    r.seg_wide[...] = jnp.transpose(jnp.broadcast_to(ids, (128, length)))
+    spread_a.begin(0)
+    spread_a.begin_beside(0)
 
     total = r.small_mine[...]
-    for at, made in enumerate(small_dp):
-        made.wait_recv()
-        total = total + r.small_dp[at]
-    r.small_sum[...] = total
-    for made in small_group:
-        made.start()
     for at, made in enumerate(small_group):
         made.wait_recv()
         total = total + jnp.where(
             lax.broadcasted_iota(jnp.int32, total.shape, 0) < 6, r.small_group[at], 0.0
         )
-    r.vecs[...] = total
+    r.small_sum[...] = total
+    for made in small_dp:
+        made.start()
+    for half in (1, 2):
+        spread_a.begin(half)
+        spread_a.begin_beside(half)
+    for chunk in range(CHUNKS):
+        given_rows.give(chunk)
+    for spread in (spread_b, spread_c):
+        for half in range(2):
+            spread.begin(half)
+    for spread in (spread_a, spread_b, spread_c):
+        spread.keep_own()
+
     gain_one, shift_one, gain_two, shift_two, bias_out, bias_fc2 = range(6)
 
     def vec(at):
         return r.vecs[at : at + 1, :]
 
+    def normalise(first):
+        @pl.loop(0, num_blocks // 2)
+        def first_norm(at):
+            rows = rows_at((at + first * (num_blocks // 2)) * BLOCK, BLOCK)
+            low = layer_norm(r.rows_all[rows, :].astype(F32), vec(gain_one), vec(shift_one))
+            r.normed[rows, :] = low.astype(BF)
+
+    frame_rows.hand_over(0)
     spread_a.forward(0)
-    frame_rows.hand_over(0)
+    for at, made in enumerate(small_dp):
+        made.wait_recv()
+        total = total + r.small_dp[at]
+    r.vecs[...] = total
+    frame_rows.await_sibling()
+    normalise(upper)
+    frame_rows.hand_over(1)
     spread_a.forward(1)
-    spread_b.begin_beside()
-    spread_c.begin_beside()
-    frame_rows.hand_over(1)
-    frame_rows.await_sibling()
-    spread_a.end()
+    frame_rows.hand_over(2)
+    spread_a.forward(2)
+    for spread in (spread_b, spread_c):
+        for half in range(2):
+            spread.begin_beside(half)
+    frame_rows.await_corner()
+    normalise(1 - upper)
+    spread_a.end((0, 1))
 
     @pl.loop(0, num_blocks)
     def project(at):
-        spot = lax.rem(at + upper * (num_blocks // 2), num_blocks)
-        rows = rows_at(spot * BLOCK, BLOCK)
-
-        @pl.when(at == num_blocks // 2)
-        def from_across():
-            frame_rows.hand_over(2)
-            frame_rows.await_corner()
-
-        low = layer_norm(
-            r.rows_all[rows, :].astype(F32), vec(gain_one), vec(shift_one)
-        ).astype(BF)
-        r.normed[rows, :] = low
-        made = dot_nn(low, flat_weight(r.full_a, r.wide)[:, :qkv])
+        rows = rows_at(at * BLOCK, BLOCK)
+        low = r.normed[rows, :]
+        made = dot_nn(low, flat_weight(r.full_a, r.wide, 0, qkv))
         made_query = (made[:, :heads_width] + r.vecs[7:8, 0:heads_width]).astype(BF)
         r.query[rows, :] = made_query * jnp.asarray(0.125, BF)
         r.keys[rows, :] = made[:, heads_width : 2 * heads_width].astype(BF)
@@ -404,6 +458,7 @@
         r.values[rows, :] = made_values
         r.turned[:, rows] = jnp.transpose(made_values)
 
+    spread_a.end((2,))
     sum_one = RowSum(links, r.part_one, r.side_one, r.home_one, r.far_one)
     spread_two = RowSpread(links, r.normed_own, r.normed_two)
 
@@ -426,7 +481,7 @@
             r.stats[spot, head : head + 1, :] = top + jnp.log(whole)
         out = jnp.transpose(jnp.concatenate(made, axis=0)).astype(BF)
         r.mixed[rows, :] = out
-        r.part_one[rows, :] = dot_nt(out, flat_weight(r.full_a, r.wide)[:, qkv:]).astype(BF)
+        r.part_one[rows, :] = dot_nt(out, flat_weight(r.full_a, r.wide, qkv)).astype(BF)
 
         def after(step, core=None):
             return pl.when((at == step) if core is None else ((at == step) & (me % 2 == core)))
@@ -476,6 +531,10 @@
         @after(4)
         def weights_second():
             spread_b.forward(1)
+
+        @after(5)
+        def weights_third():
+            spread_c.forward(0)
 
     sum_one.begin_home()
     given_rows.hand_over(2)
@@ -485,13 +544,13 @@
         r.middle[cut, :] = row
         r.normed_own[cut, :] = layer_norm(row, vec(gain_two), vec(shift_two)).astype(BF)
         spread_two.give(chunk)
-        if chunk < 2:
-            spread_c.forward(chunk)
+        if chunk == 1:
+            spread_c.forward(1)
     links.sent(sum_one.far_in + frame_rows.corner_in)
     given_rows.await_sibling()
     given_rows.await_corner()
-    spread_b.end()
-    spread_c.end()
+    spread_b.end((0, 1))
+    spread_c.end((0, 1))
 
     sum_two = RowSum(links, r.part_two, r.side_two, r.home_two, r.far_two)
     sum_three = RowSum(links, r.normed_two, r.side_three, r.home_three, r.far_three)
@@ -529,8 +588,7 @@
             ref[rows_too, :] = low[block // CHUNKS :]
 
         hidden = dot_nn(both(r.normed_two), flat_weight(r.full_b, r.wide)) + r.vecs[6:7, :]
-        below = 0.5 + 0.5 * lax.erf(hidden * 0.7071067811865476)
-        density = 0.3989422804014327 * jnp.exp(-0.5 * hidden * hidden)
+        below, density = normal_parts(hidden)
         put(r.active, hidden * below)
         grad_active = dot_nn(both(r.given_all), flat_weight(r.full_c, r.wide))
         back = (grad_active * (below + hidden * density)).astype(BF)
@@ -569,16 +627,17 @@
         r.small_grads[bias_out : bias_out + 1, :] += column_sum(low.astype(F32))
         r.small_grads[bias_fc2 : bias_fc2 + 1, :] += column_sum(given)
 
-    second_norm_back(0)
-
-    @pl.loop(0, width // block)
     def weigh_one(at):
         columns = rows_at(at * block, block)
         made = dot_tn(r.normed_two[:, columns], r.grad_hidden[...])
         split_rows(made, r.grads_b, at * block, r.wide)
 
+    second_norm_back(0)
+    weigh_one(0)
+    second_norm_back(1)
+    weigh_one(1)
     scatter_b.begin()
-    second_norm_back(1)
+    second_norm_back(2)
 
     @pl.loop(0, width // block)
     def weigh_two(at):
@@ -587,7 +646,6 @@
         split_rows(made, r.grads_c, at * block, r.wide)
 
     scatter_c.begin()
-    second_norm_back(2)
     links.sent(spread_two.corner_in)
 
     @pl.loop(0, 4)
@@ -650,7 +708,7 @@
         spot = lax.rem(at + upper * (num_blocks // 2), num_blocks)
         rows = rows_at(spot * BLOCK, BLOCK)
         asked = r.query[rows, :]
-        given = dot_nn(r.rows_all[rows, :], flat_weight(r.full_a, r.wide)[:, qkv:]).astype(BF)
+        given = dot_nn(r.rows_all[rows, :], flat_weight(r.full_a, r.wide, qkv)).astype(BF)
         joint = jnp.transpose(given.astype(F32) * r.mixed[rows, :].astype(F32))
         keys_ids = jnp.concatenate([r.seg_wide[...]] * (BLOCK // 128), axis=1)
         query_ids = r.seg_row[0:1, rows].astype(F32)
@@ -676,19 +734,25 @@
     links.sent(sum_one.side_in + sum_one.home_in)
     sum_four = RowSum(links, r.part_one, r.side_one, r.home_one, r.far_one)
 
-    @pl.loop(0, 4)
-    def project_back(at):
-        rows = rows_at((me ^ (3 - at)) * block, block)
+    def join(rows):
         low_keys = r.grad_keys[rows, :].astype(BF)
         low_values = r.grad_values[rows, :].astype(BF)
         low_query = r.grad_proj[rows, :heads_width]
         whole = jnp.concatenate([low_query, low_keys, low_values], axis=1)
         r.grad_proj[rows, :] = whole
-        made = dot_nt(whole, flat_weight(r.full_a, r.wide)[:, :qkv])
-        r.part_one[rows, :] = made.astype(BF)
         wide_sum = column_sum(whole.astype(F32))
         r.small_grads[7:8, 0:heads_width] += wide_sum[:, 0:heads_width]
         r.small_grads[7:8, LANE_GAP : LANE_GAP + heads_width] += wide_sum[:, 2 * heads_width :]
+
+    def push(rows):
+        made = dot_nt(r.grad_proj[rows, :], flat_weight(r.full_a, r.wide, 0, qkv))
+        r.part_one[rows, :] = made.astype(BF)
+
+    @pl.loop(0, 2)
+    def project_remote(at):
+        rows = rows_at((me ^ (3 - at)) * block, block)
+        join(rows)
+        push(rows)
 
         @pl.when(at == 0)
         def corner_done():
@@ -699,9 +763,9 @@
             for chunk in range(CHUNKS):
                 sum_four.pass_on(chunk)
 
-        @pl.when(at == 2)
-        def sibling_done():
-            sum_four.begin_home()
+    @pl.loop(0, 2)
+    def join_near(at):
+        join(rows_at((me ^ at) * block, block))
 
     scatter_a = GradScatter(links, r.grads_a, r.beside_a, r.landed_a, r.out_a)
 
@@ -718,6 +782,12 @@
         split_rows(both, r.grads_a, at * block, r.wide)
 
     scatter_a.begin()
+
+    @pl.loop(0, 2)
+    def project_near(at):
+        push(rows_at((me ^ (1 - at)) * block, block))
+
+    sum_four.begin_home()
     for chunk in range(CHUNKS):
         cut = sum_three.cut(chunk)
         row = r.middle[cut, :] + (sum_three.total(chunk) + vec(bias_fc2))
@@ -758,10 +828,10 @@
     for at, made in enumerate(back_dp):
         made.wait_recv()
         total = total + r.small_dp[at]
-    own = (dp * 4 + me) * (width // (4 * num_dp))
-    r.small_out[0:6, :] = pltpu.roll(total[0:6, :], lax.rem(width - own, width), 1)
-    own = dp * (HD // num_dp)
-    r.small_out[6:8, :] = pltpu.roll(total[6:8, :], lax.rem(width - own, width), 1)
+    start = (dp * 4 + me) * own
+    r.small_out[0:6, :] = pltpu.roll(total[0:6, :], lax.rem(width - start, width), 1)
+    start = dp * share
+    r.small_out[6:8, :] = pltpu.roll(total[6:8, :], lax.rem(width - start, width), 1)
     links.finish()
 
 
@@ -769,27 +839,30 @@
     far = num_dp // 2
     smalls = 2 * (num_dp - 1 + 3)
     spreads = 4 * 3 * CHUNKS
-    weights = 3 * 2 * (2 * far - 1)
+    weights = (3 + 2 + 2) * (2 * far - 1)
     sums = 4 * 3 * CHUNKS
     scatters = 3 * (2 * far - 1)
     return smalls + spreads + weights + sums + scatters
 
 
-def layer(num_dp, seg, frames, cotangent, small, shard_a, shard_b, shard_c):
+def layer(num_dp, seg, frames, cotangent, vecs, proj_bias, fc1_bias, in_weight, out_weight, shard_b, shard_c):
     block, width = frames.shape
-    length, slab = 4 * block, shard_a.shape[0]
+    length, slab = 4 * block, shard_b.shape[0]
     heads_width = width // 4
     num_blocks = length // BLOCK
-    vmem, hbm = pl.BlockSpec(memory_space=pltpu.VMEM), pl.BlockSpec(memory_space=pl.ANY)
+    vmem = pl.BlockSpec(memory_space=pltpu.VMEM)
     inputs = [
         ("seg_row", seg, vmem),
         ("frames", frames, vmem),
         ("cotangent", cotangent, vmem),
-        ("small", small, vmem),
-        ("shard_a", shard_a, vmem),
+        ("proj_bias", proj_bias, vmem),
+        ("fc1_bias", fc1_bias, vmem),
+        ("in_weight", in_weight, vmem),
+        ("out_weight", out_weight, vmem),
         ("shard_b", shard_b, vmem),
         ("shard_c", shard_c, vmem),
     ]
+    inputs += [(f"vec_{at}", value, vmem) for at, value in enumerate(vecs)]
     outputs = [
         ("output", (block, width), BF),
         ("grad_frames", (block, width), F32),
@@ -831,6 +904,7 @@
         ("normed_own", (block, width), BF),
         ("attended_own", (block, width), BF),
         ("vecs", (8, width), F32),
+        ("shard_a", (slab, width), BF),
         ("wide", (width if slab % 16 else 8, width), F32),
     ]
     for name in ("small_mine", "small_sum", "small_grads", "small_total"):
@@ -854,6 +928,63 @@
     )(*[value for _, value, _ in inputs])
 
 
+def unpack_kernel(own, share, output, grad_frames, grads_a, grads_b, grads_c, sums, output_too, grad_frames_too, g_in, g_proj, g_out, grads_b_too, g_fc1b, grads_c_too, vec_0, vec_1, vec_2, vec_3, vec_4, vec_5, sems):
+    pairs = (
+        (output, output_too),
+        (grad_frames, grad_frames_too),
+        (grads_b, grads_b_too),
+        (grads_c, grads_c_too),
+    )
+    copies = [pltpu.make_async_copy(*pair, sems.at[at]) for at, pair in enumerate(pairs)]
+    for made in copies:
+        made.start()
+    heads_width = g_in.shape[2]
+    for at in range(3):
+        g_in[at] = grads_a[:, at * heads_width : (at + 1) * heads_width]
+    g_out[...] = jnp.transpose(grads_a[:, 3 * heads_width :])
+    for at, vec in enumerate((vec_0, vec_1, vec_2, vec_3, vec_4, vec_5)):
+        vec[...] = sums[at : at + 1, 0:own]
+    width = sums.shape[1]
+    pieces = [
+        pltpu.roll(sums[...], (width - at * HD) % width, 1)[6:7, 0:128] for at in range(width // HD)
+    ]
+    pieces.append(jnp.zeros((16 - len(pieces), 128), F32))
+    g_fc1b[...] = jnp.transpose(jnp.concatenate(pieces, axis=0))[0:share, 0 : width // HD]
+    for head in range(heads_width // HD):
+        for at in range(2):
+            start = at * LANE_GAP + head * HD
+            piece = pltpu.roll(sums[...], (width - start) % width, 1)
+            g_proj[head, at : at + 1, :] = piece[7:8, 0:share]
+    for made in copies:
+        made.wait()
+
+
+def unpack(own, share, results):
+    output, grad_frames, grads_a, grads_b, grads_c, sums = results
+    slab, width = grads_a.shape
+    heads_width = width // 4
+    vmem, hbm = pl.BlockSpec(memory_space=pltpu.VMEM), pl.BlockSpec(memory_space=pl.ANY)
+    shapes = [
+        (output.shape, BF, hbm),
+        (grad_frames.shape, F32, hbm),
+        ((3, slab, heads_width), F32, vmem),
+        ((heads_width // HD, 2, share), F32, vmem),
+        ((heads_width, slab), F32, vmem),
+        ((slab, width), F32, hbm),
+        ((share, width // HD), F32, vmem),
+        ((slab, width), F32, hbm),
+    ] + [((1, own), F32, vmem)] * 6
+    return pl.pallas_call(
+        functools.partial(unpack_kernel, own, share),
+        out_shape=[jax.ShapeDtypeStruct(shape, kind) for shape, kind, _ in shapes],
+        in_specs=[vmem] * 6,
+        out_specs=[spec for _, _, spec in shapes],
+        scratch_shapes=[pltpu.SemaphoreType.DMA((4,))],
+        compiler_params=pltpu.CompilerParams(vmem_limit_bytes=VMEM_BYTES),
+        name="unpack",
+    )(*results)
+
+
 def on_device(
     num_dp,
     frames,
@@ -872,44 +1003,40 @@
     fc2_bias,
     cotangent,
 ):
-    width = frames.shape[1]
     slab, _, heads_width = in_weight.shape
-    heads = heads_width // HD
-    own = norm1_gain.shape[0]
-    share = HD // num_dp
-    vecs = jnp.stack([norm1_gain, norm1_shift, norm2_gain, norm2_shift, out_bias, fc2_bias])
-    vecs = jnp.pad(vecs, ((0, 0), (0, width - own)))
-    fc1_row = jnp.pad(fc1_bias.astype(F32), ((0, 0), (0, HD - share))).reshape(1, width)
-    proj_row = jnp.pad(
-        proj_bias.astype(F32),
-        ((0, 0), (0, LANE_GAP // HD - heads), (0, HD - share)),
-    ).reshape(1, 2 * LANE_GAP)
-    proj_row = jnp.pad(proj_row, ((0, 0), (0, width - 2 * LANE_GAP)))
-    small = jnp.concatenate([vecs, fc1_row, proj_row], axis=0)
-    shard_a = jnp.concatenate([in_weight.reshape(slab, 3 * heads_width), out_weight.T], axis=1)
-    output, grad_frames, g_a, g_b, g_c, sums = layer(
-        num_dp, segments, frames, cotangent, small, shard_a, fc1_weight, fc2_weight.T
+    vecs = [norm1_gain, norm1_shift, norm2_gain, norm2_shift, out_bias, fc2_bias]
+    results = layer(
+        num_dp,
+        segments,
+        frames,
+        cotangent,
+        [value[None] for value in vecs],
+        proj_bias.transpose(1, 0, 2),
+        fc1_bias.T,
+        in_weight.transpose(1, 0, 2),
+        out_weight,
+        fc1_weight,
+        fc2_weight.T,
     )
-    g_in = g_a[:, : 3 * heads_width].reshape(slab, 3, heads_width)
-    g_out = g_a[:, 3 * heads_width :].T
-    mine = sums[0:6, :own]
-    g_fc1b = sums[6].reshape(-1, HD)[:, :share]
-    g_proj = sums[7, : 2 * LANE_GAP].reshape(2, LANE_GAP // HD, HD)[:, :heads, :share]
+    output, grad_frames, g_in, g_proj, g_out, g_b, g_fc1b, g_c, *rows = unpack(
+        norm1_gain.shape[0], HD // num_dp, results
+    )
+    rows = [row[0] for row in rows]
     return (
         output,
         grad_frames,
-        mine[0],
-        mine[1],
-        g_in,
-        g_proj,
+        rows[0],
+        rows[1],
+        g_in.transpose(1, 0, 2),
+        g_proj.transpose(1, 0, 2),
         g_out,
-        mine[4],
-        mine[2],
-        mine[3],
+        rows[4],
+        rows[2],
+        rows[3],
         g_b,
-        g_fc1b,
+        g_fc1b.T,
         g_c.T,
-        mine[5],
+        rows[5],
     )
 
 

time: 185 us -> 159 us (0.86)
  local copies, waits for them, and re-layouts: 15.9 us -> 0 us
  Pallas kernels: 166 us -> 157 us
    pallas_call x1, Pallas kernels: 166 us -> 153 us  [layer(): pl.pallas_call(functools.partial(layer_kernel, num_dp, names), out_shape=...]
    unnamed x20 -> x0, local copies, waits for them, and re-layouts: 9.65 us -> none
    pallas_call x0 -> x1, Pallas kernels: none -> 3.88 us  [unpack(): pl.pallas_call(functools.partial(unpack_kernel, own, share), out_shape=[j...]
    slice x4 -> x0, local copies, waits for them, and re-layouts: 2.59 us -> none  [the longest x2 1.11 us: on_device(): g_in = g_a[:, :3 * heads_width].reshape(slab, 3, heads_width)]
where the time goes in v3:
time: 159 us; the launch traced here: 158 us
  Pallas kernels  157 us (99%)
    pallas_call x1, Pallas kernels, layer(): pl.pallas_call(functools.partial(layer_kernel, num_dp, names), out_shape=...  153 us
    pallas_call x1, Pallas kernels, unpack(): pl.pallas_call(functools.partial(unpack_kernel, own, share), out_shape=[j...  3.88 us

profile of v3, /device:TPU:0, one launch (start us, length us, event | category | flops | bytes accessed | tf_op | source)
XLA Modules:
  0.0 157.8 jit_solution(8309954434887043249)
XLA Ops:
  0.7 153.1 %layer.1 = (bf16[384,768]{1,0:T(8,128)(2,1)}, f32[384,768]{1,0:T(8,128)}, f32[96,768]{1,0:T(8,128)}, f32[96,768]{1,0:T(8,128)}, f32[96,768]{1,0:T(8,128)}, /*index=5*/f32[8,768]{1,0:T(8,128)}) custom-call(s32[1,1536]{1,0:T(1,128)} %refs_0_.1, bf16[384,768]{1,0:T(8,128)(2,1)} %refs_1_.1, bf16[384,768]{1,0:T(8,128)(2,1)} %refs_2_.1, ...), custom_call_target="tpu_custom_call" | custom-call | tf_op jit(solution)/shard_map/layer/pallas_call | solution.py:917
  153.7 3.9 %unpack.1 = (bf16[384,768]{1,0:T(8,128)(2,1)}, f32[384,768]{1,0:T(8,128)}, f32[3,96,192]{2,1,0:T(8,128)}, f32[3,2,8]{2,1,0:T(2,128)}, f32[192,96]{1,0:T(8,128)},...) custom-call(bf16[384,768]{1,0:T(8,128)(2,1)} %get-tuple-element.34.o, ...), custom_call_target="tpu_custom_call" | custom-call | tf_op jit(solution)/shard_map/unpack/pallas_call | solution.py:977

commit v4 on v3

--- a/solution.py
+++ b/solution.py
@@ -50,14 +50,8 @@
 
 
 def normal_parts(hidden):
-    bell = jnp.exp(-0.5 * hidden * hidden)
-    near = 1.0 / (1.0 + 0.23164189 * jnp.abs(hidden))
-    tail = near * (
-        0.127414796
-        + near * (-0.142248368 + near * (0.7107068705 + near * (-0.7265760135 + near * 0.5307027145)))
-    )
-    above = tail * bell
-    return jnp.where(hidden < 0.0, above, 1.0 - above), 0.3989422804014327 * bell
+    below = 0.5 + 0.5 * lax.erf(hidden * 0.7071067811865476)
+    return below, 0.3989422804014327 * jnp.exp(-0.5 * hidden * hidden)
 
 
 def column_sum(block):
@@ -260,7 +254,11 @@
 
 
 class GradScatter:
-    def __init__(self, links, grads, beside, landed, result):
+    def __init__(self, links, grads, beside, landed, result, start=0, stop=None):
+        stop = stop or grads.shape[2]
+        lanes = pl.ds(start, stop - start)
+        grads, beside, landed = (ref.at[:, :, lanes] for ref in (grads, beside, landed))
+        result = result.at[:, lanes]
         self.links, self.grads, self.beside = links, grads, beside
         self.landed, self.result = landed, result
         self.slab = beside.shape[1]
@@ -310,17 +308,17 @@
     return wide[:, start:stop].astype(BF)
 
 
-def split_rows(value, grads, start, wide):
+def split_rows(value, grads, start, wide, lane=0):
     count, slab, width = grads.shape
-    rows = value.shape[0]
+    rows, columns = value.shape
+    lanes = slice(lane, lane + columns)
     if slab % 16 == 0:
-        grads[pl.ds(start // slab, rows // slab)] = value.astype(BF).reshape(
-            rows // slab, slab, width
-        )
+        low = value.astype(BF).reshape(rows // slab, slab, columns)
+        grads[pl.ds(start // slab, rows // slab), :, lanes] = low
         return
-    wide[0:rows, :] = value
+    wide[0:rows, lanes] = value
     for at in range(rows // slab):
-        grads[start // slab + at] = wide[at * slab : (at + 1) * slab, :].astype(BF)
+        grads[start // slab + at, :, lanes] = wide[at * slab : (at + 1) * slab, lanes].astype(BF)
 
 
 def turn(value):
@@ -411,6 +409,7 @@
     for spread in (spread_b, spread_c):
         for half in range(2):
             spread.begin(half)
+            spread.begin_beside(half)
     for spread in (spread_a, spread_b, spread_c):
         spread.keep_own()
 
@@ -438,9 +437,6 @@
     spread_a.forward(1)
     frame_rows.hand_over(2)
     spread_a.forward(2)
-    for spread in (spread_b, spread_c):
-        for half in range(2):
-            spread.begin_beside(half)
     frame_rows.await_corner()
     normalise(1 - upper)
     spread_a.end((0, 1))
@@ -459,6 +455,7 @@
         r.turned[:, rows] = jnp.transpose(made_values)
 
     spread_a.end((2,))
+    spread_b.forward(0)
     sum_one = RowSum(links, r.part_one, r.side_one, r.home_one, r.far_one)
     spread_two = RowSpread(links, r.normed_own, r.normed_two)
 
@@ -491,10 +488,6 @@
             sum_one.side_in[0].start()
             sum_one.side_in[1].start()
 
-        @after(0)
-        def weights_first():
-            spread_b.forward(0)
-
         @after(1, 0)
         def lower_second():
             sum_one.pass_on(0)
@@ -508,6 +501,7 @@
         @after(1)
         def rows_first():
             given_rows.hand_over(0)
+            spread_b.forward(1)
 
         @after(2, 0)
         def lower_third():
@@ -530,26 +524,61 @@
 
         @after(4)
         def weights_second():
-            spread_b.forward(1)
-
-        @after(5)
-        def weights_third():
             spread_c.forward(0)
 
     sum_one.begin_home()
     given_rows.hand_over(2)
-    for chunk in range(CHUNKS):
-        cut = sum_one.cut(chunk)
-        row = r.frames[cut, :].astype(F32) + (sum_one.total(chunk) + vec(bias_out))
-        r.middle[cut, :] = row
-        r.normed_own[cut, :] = layer_norm(row, vec(gain_two), vec(shift_two)).astype(BF)
-        spread_two.give(chunk)
-        if chunk == 1:
-            spread_c.forward(1)
+    r.grad_keys[...] = jnp.zeros_like(r.grad_keys)
+    r.grad_values[...] = jnp.zeros_like(r.grad_values)
+
+    @pl.loop(0, num_blocks)
+    def turn_keys(at):
+        rows = rows_at(at * BLOCK, BLOCK)
+        r.turned[:, rows] = jnp.transpose(r.keys[rows, :])
+
+    spread_b.end((0, 1))
+
+    def pair_rows(chunk, member):
+        start = chunk * (block // CHUNKS)
+        return (
+            rows_at(member * block + start, block // CHUNKS),
+            rows_at((member ^ 1) * block + start, block // CHUNKS),
+        )
+
+    def both(ref, pair):
+        return jnp.concatenate([ref[rows, :] for rows in pair], axis=0)
+
+    def put(ref, pair, value):
+        low = value.astype(BF)
+        ref[pair[0], :] = low[: block // CHUNKS]
+        ref[pair[1], :] = low[block // CHUNKS :]
+
+    def hide(pair):
+        hidden = dot_nn(both(r.normed_two, pair), flat_weight(r.full_b, r.wide)) + r.vecs[6:7, :]
+        below, density = normal_parts(hidden)
+        put(r.active, pair, hidden * below)
+        put(r.part_two, pair, below + hidden * density)
+
+    @pl.loop(0, CHUNKS)
+    def second_norm(at):
+        for chunk in range(CHUNKS):
+
+            @pl.when(at == chunk)
+            def rows_of(chunk=chunk):
+                cut = sum_one.cut(chunk)
+                row = r.frames[cut, :].astype(F32) + (sum_one.total(chunk) + vec(bias_out))
+                r.middle[cut, :] = row
+                r.normed_own[cut, :] = layer_norm(row, vec(gain_two), vec(shift_two)).astype(BF)
+                spread_two.give(chunk)
+                if chunk == 0:
+                    spread_c.forward(1)
+                spread_two.sibling_in[chunk].wait_recv()
+
+        hide(pair_rows(at, me))
+
     links.sent(sum_one.far_in + frame_rows.corner_in)
     given_rows.await_sibling()
     given_rows.await_corner()
-    spread_b.end((0, 1))
     spread_c.end((0, 1))
 
     sum_two = RowSum(links, r.part_two, r.side_two, r.home_two, r.far_two)
@@ -564,36 +593,25 @@
         for chunk in range(CHUNKS):
 
             @when_at(2 * chunk)
-            def near(chunk=chunk):
-                spread_two.sibling_in[chunk].wait_recv()
+            def bring(chunk=chunk):
+                spread_two.hand_over(chunk)
 
             @when_at(2 * chunk + 1)
             def remote(chunk=chunk):
-                spread_two.hand_over(chunk)
                 if chunk:
                     sum_two.pass_on(chunk - 1)
                 spread_two.corner_in[chunk].wait_recv()
 
-        chunk_start = (at // 2) * (block // CHUNKS)
-        member = me ^ (2 * (at % 2))
-        rows = rows_at(member * block + chunk_start, block // CHUNKS)
-        rows_too = rows_at((member ^ 1) * block + chunk_start, block // CHUNKS)
-
-        def both(ref):
-            return jnp.concatenate([ref[rows, :], ref[rows_too, :]], axis=0)
-
-        def put(ref, value):
-            low = value.astype(BF)
-            ref[rows, :] = low[: block // CHUNKS]
-            ref[rows_too, :] = low[block // CHUNKS :]
-
-        hidden = dot_nn(both(r.normed_two), flat_weight(r.full_b, r.wide)) + r.vecs[6:7, :]
-        below, density = normal_parts(hidden)
-        put(r.active, hidden * below)
-        grad_active = dot_nn(both(r.given_all), flat_weight(r.full_c, r.wide))
-        back = (grad_active * (below + hidden * density)).astype(BF)
-        put(r.grad_hidden, back)
-        put(r.part_two, dot_nt(back, flat_weight(r.full_b, r.wide)))
+        pair = pair_rows(at // 2, me ^ (2 * (at % 2)))
+
+        @pl.when(at % 2 == 1)
+        def remote_first():
+            hide(pair)
+
+        grad_active = dot_nn(both(r.given_all, pair), flat_weight(r.full_c, r.wide))
+        back = (grad_active * both(r.part_two, pair).astype(F32)).astype(BF)
+        put(r.grad_hidden, pair, back)
+        put(r.part_two, pair, dot_nt(back, flat_weight(r.full_b, r.wide)))
         r.small_grads[6:7, :] += column_sum(back.astype(F32))
 
         for chunk in range(CHUNKS):
@@ -632,19 +650,19 @@
         made = dot_tn(r.normed_two[:, columns], r.grad_hidden[...])
         split_rows(made, r.grads_b, at * block, r.wide)
 
+    def weigh_two(at):
+        columns = rows_at(at * block, block)
+        made = dot_tn(r.given_all[:, columns], r.active[...])
+        split_rows(made, r.grads_c, at * block, r.wide)
+
     second_norm_back(0)
     weigh_one(0)
     second_norm_back(1)
     weigh_one(1)
     scatter_b.begin()
+    weigh_two(0)
     second_norm_back(2)
-
-    @pl.loop(0, width // block)
-    def weigh_two(at):
-        columns = rows_at(at * block, block)
-        made = dot_tn(r.given_all[:, columns], r.active[...])
-        split_rows(made, r.grads_c, at * block, r.wide)
-
+    weigh_two(1)
     scatter_c.begin()
     links.sent(spread_two.corner_in)
 
@@ -662,14 +680,6 @@
         def sibling_done():
             sum_three.begin_home()
 
-    r.grad_keys[...] = jnp.zeros_like(r.grad_keys)
-    r.grad_values[...] = jnp.zeros_like(r.grad_values)
-
-    @pl.loop(0, num_blocks)
-    def turn_keys(at):
-        rows = rows_at(at * BLOCK, BLOCK)
-        r.turned[:, rows] = jnp.transpose(r.keys[rows, :])
-
     spread_three.await_sibling()
 
     @pl.loop(0, num_blocks)
@@ -682,18 +692,18 @@
             for chunk in range(CHUNKS):
                 sum_three.pass_on(chunk)
             spread_three.hand_over(0)
+            spread_three.hand_over(1)
             scatter_b.pass_on(1)
             scatter_b.pass_on(2)
 
         @when_at(2)
         def second_service():
-            spread_three.hand_over(1)
+            spread_three.hand_over(2)
             for step in range(3, links.num_far):
                 scatter_b.pass_on(step)
 
         @when_at(3)
         def third_service():
-            spread_three.hand_over(2)
             spread_three.await_corner()
 
         @when_at(4)
@@ -767,43 +777,60 @@
     def join_near(at):
         join(rows_at((me ^ at) * block, block))
 
-    scatter_a = GradScatter(links, r.grads_a, r.beside_a, r.landed_a, r.out_a)
+    middle_lane = width // 2
+    scatter_a = [
+        GradScatter(links, r.grads_a, r.beside_a, r.landed_a, r.out_a, *lanes)
+        for lanes in ((0, middle_lane), (middle_lane, width))
+    ]
 
     @pl.loop(0, width // block)
     def weigh_in(at):
         columns = rows_at(at * block, block)
-        both = jnp.concatenate(
+        made = dot_tn(r.normed[:, columns], r.grad_proj[:, 0:middle_lane])
+        split_rows(made, r.grads_a, at * block, r.wide, 0)
+
+    scatter_a[0].begin()
+
+    @pl.loop(0, width // block)
+    def weigh_in_too(at):
+        columns = rows_at(at * block, block)
+        made = jnp.concatenate(
             [
-                dot_tn(r.normed[:, columns], r.grad_proj[...]),
+                dot_tn(r.normed[:, columns], r.grad_proj[:, middle_lane:qkv]),
                 dot_tn(r.rows_all[:, columns], r.mixed[...]),
             ],
             axis=1,
         )
-        split_rows(both, r.grads_a, at * block, r.wide)
-
-    scatter_a.begin()
+        split_rows(made, r.grads_a, at * block, r.wide, middle_lane)
+
+    scatter_a[1].begin()
 
     @pl.loop(0, 2)
     def project_near(at):
         push(rows_at((me ^ (1 - at)) * block, block))
 
     sum_four.begin_home()
-    for chunk in range(CHUNKS):
-        cut = sum_three.cut(chunk)
-        row = r.middle[cut, :] + (sum_three.total(chunk) + vec(bias_fc2))
-        r.output[cut, :] = row.astype(BF)
-    for step in range(1, links.num_far):
-        scatter_a.pass_on(step)
-    scatter_b.end()
-    scatter_c.end()
-
-    for chunk in range(CHUNKS):
+    def first_norm_back(chunk):
         cut = sum_four.cut(chunk)
         grad = sum_four.total(chunk)
         back, unit = layer_norm_back(r.frames[cut, :].astype(F32), grad, vec(gain_one))
         r.grad_frames[cut, :] = r.grad_middle[cut, :] + back
         r.small_grads[gain_one : gain_one + 1, :] += column_sum(grad * unit)
         r.small_grads[shift_one : shift_one + 1, :] += column_sum(grad)
+
+    scatter_b.end()
+    scatter_a[0].pass_on(1)
+    first_norm_back(0)
+    for step in range(2, links.num_far):
+        scatter_a[0].pass_on(step)
+    for chunk in range(CHUNKS):
+        cut = sum_three.cut(chunk)
+        row = r.middle[cut, :] + (sum_three.total(chunk) + vec(bias_fc2))
+        r.output[cut, :] = row.astype(BF)
+    first_norm_back(1)
+    scatter_a[1].pass_on(1)
+    scatter_a[1].pass_on(2)
+    first_norm_back(2)
 
     back_group = [
         links.copy(r.small_grads, r.small_group_back.at[at], device)
@@ -815,6 +842,8 @@
     ]
     for made in back_group:
         made.start()
+    for step in range(3, links.num_far):
+        scatter_a[1].pass_on(step)
     total = r.small_grads[...]
     for at, made in enumerate(back_group):
         made.wait_recv()
@@ -824,7 +853,9 @@
     r.small_total[...] = total
     for made in back_dp:
         made.start()
-    scatter_a.end()
+    scatter_c.end()
+    for scatter in scatter_a:
+        scatter.end()
     for at, made in enumerate(back_dp):
         made.wait_recv()
         total = total + r.small_dp[at]
@@ -841,7 +872,7 @@
     spreads = 4 * 3 * CHUNKS
     weights = (3 + 2 + 2) * (2 * far - 1)
     sums = 4 * 3 * CHUNKS
-    scatters = 3 * (2 * far - 1)
+    scatters = 4 * (2 * far - 1)
     return smalls + spreads + weights + sums + scatters
 
 

time: 159 us -> 151 us (0.950)
  Pallas kernels: 157 us -> 150 us
    pallas_call x1, Pallas kernels: 153 us -> 146 us  [layer(): pl.pallas_call(functools.partial(layer_kernel, num_dp, names), out_shape=...]
where the time goes in v4:
time: 151 us
  Pallas kernels  150 us (99%)
    pallas_call x1, Pallas kernels, layer(): pl.pallas_call(functools.partial(layer_kernel, num_dp, names), out_shape=...  146 us
    pallas_call x1, Pallas kernels, unpack(): pl.pallas_call(functools.partial(unpack_kernel, own, share), out_shape=[j...  3.88 us

profile of v4, /device:TPU:0, one launch (start us, length us, event | category | flops | bytes accessed | tf_op | source)
XLA Modules:
  0.0 151.2 jit_solution(7874123256795032461)
XLA Ops:
  0.7 146.5 %layer.1 = (bf16[384,768]{1,0:T(8,128)(2,1)}, f32[384,768]{1,0:T(8,128)}, f32[96,768]{1,0:T(8,128)}, f32[96,768]{1,0:T(8,128)}, f32[96,768]{1,0:T(8,128)}, /*index=5*/f32[8,768]{1,0:T(8,128)}) custom-call(s32[1,1536]{1,0:T(1,128)} %refs_0_.1, bf16[384,768]{1,0:T(8,128)(2,1)} %refs_1_.1, bf16[384,768]{1,0:T(8,128)(2,1)} %refs_2_.1, ...), custom_call_target="tpu_custom_call" | custom-call | tf_op jit(solution)/shard_map/layer/pallas_call | solution.py:948
  147.2 3.9 %unpack.1 = (bf16[384,768]{1,0:T(8,128)(2,1)}, f32[384,768]{1,0:T(8,128)}, f32[3,96,192]{2,1,0:T(8,128)}, f32[3,2,8]{2,1,0:T(2,128)}, f32[192,96]{1,0:T(8,128)},...) custom-call(bf16[384,768]{1,0:T(8,128)(2,1)} %get-tuple-element.34.o, ...), custom_call_target="tpu_custom_call" | custom-call | tf_op jit(solution)/shard_map/unpack/pallas_call | solution.py:1008

commit v5 on v4

--- a/solution.py
+++ b/solution.py
@@ -13,6 +13,7 @@
 VMEM_BYTES = 62 << 20
 BLOCK = 256
 CHUNKS = 3
+DOCUMENT_LIMIT = 768
 LANE_GAP = 256
 
 
@@ -454,6 +455,28 @@
         r.values[rows, :] = made_values
         r.turned[:, rows] = jnp.transpose(made_values)
 
+    reach = (DOCUMENT_LIMIT - 2) // BLOCK + 1
+    spans = sorted(
+        {
+            min(num_blocks - 1, spot + reach) - max(0, spot - reach) + 1
+            for spot in range(num_blocks)
+        }
+    )
+
+    def by_span(spot, run):
+        first = jnp.maximum(spot - reach, 0)
+        count = jnp.minimum(spot + reach, num_blocks - 1) - first + 1
+        for span in spans:
+
+            @pl.when(count == span)
+            def this_span(span=span):
+                run(first * BLOCK, span * BLOCK)
+
+    def mask_of(rows, near, size):
+        keys_ids = jnp.concatenate([r.seg_wide[near, :]] * (BLOCK // 128), axis=1)
+        query_ids = r.seg_row[0:1, rows].astype(F32)
+        r.mask[0:size, :] = jnp.where(keys_ids == query_ids, 0.0, -1e30)
+
     spread_a.end((2,))
     spread_b.forward(0)
     sum_one = RowSum(links, r.part_one, r.side_one, r.home_one, r.far_one)
@@ -463,21 +486,24 @@
     def attend(at):
         spot = lax.rem(at + (1 - upper) * (num_blocks // 2), num_blocks)
         rows = rows_at(spot * BLOCK, BLOCK)
-        asked = r.query[rows, :]
-        keys_ids = jnp.concatenate([r.seg_wide[...]] * (BLOCK // 128), axis=1)
-        query_ids = r.seg_row[0:1, rows].astype(F32)
-        r.mask[...] = jnp.where(keys_ids == query_ids, 0.0, -1e30)
-        made = []
-        for head in range(heads):
-            scores = dot_nt(r.keys[...], head_part(asked, head)) + r.mask[...]
-            top = jnp.max(scores, axis=0, keepdims=True)
-            weights = jnp.exp(scores - top)
-            whole = column_sum(weights)
-            mixed = dot_nn(r.turned[head * HD : (head + 1) * HD, :], weights.astype(BF))
-            made.append(mixed / whole)
-            r.stats[spot, head : head + 1, :] = top + jnp.log(whole)
-        out = jnp.transpose(jnp.concatenate(made, axis=0)).astype(BF)
-        r.mixed[rows, :] = out
+
+        def mix(start, size):
+            near = rows_at(start, size)
+            mask_of(rows, near, size)
+            asked = r.query[rows, :]
+            made = []
+            for head in range(heads):
+                scores = dot_nt(r.keys[near, :], head_part(asked, head)) + r.mask[0:size, :]
+                top = jnp.max(scores, axis=0, keepdims=True)
+                weights = jnp.exp(scores - top)
+                whole = column_sum(weights)
+                given_t = r.turned[head * HD : (head + 1) * HD, near]
+                made.append(dot_nn(given_t, weights.astype(BF)) / whole)
+                r.stats[spot, head : head + 1, :] = top + jnp.log(whole)
+            r.mixed[rows, :] = jnp.transpose(jnp.concatenate(made, axis=0)).astype(BF)
+
+        by_span(spot, mix)
+        out = r.mixed[rows, :]
         r.part_one[rows, :] = dot_nt(out, flat_weight(r.full_a, r.wide, qkv)).astype(BF)
 
         def after(step, core=None):
@@ -720,26 +746,31 @@
         asked = r.query[rows, :]
         given = dot_nn(r.rows_all[rows, :], flat_weight(r.full_a, r.wide, qkv)).astype(BF)
         joint = jnp.transpose(given.astype(F32) * r.mixed[rows, :].astype(F32))
-        keys_ids = jnp.concatenate([r.seg_wide[...]] * (BLOCK // 128), axis=1)
-        query_ids = r.seg_row[0:1, rows].astype(F32)
-        r.mask[...] = jnp.where(keys_ids == query_ids, 0.0, -1e30)
         asked_heads = [head_part(asked, head) for head in range(heads)]
         given_heads = [head_part(given, head) for head in range(heads)]
-        made = []
-        for head in range(heads):
-            lanes = slice(head * BLOCK, (head + 1) * BLOCK)
-            scores = dot_nt(r.keys[...], asked_heads[head]) + r.mask[...]
-            probs = jnp.exp(scores - r.stats[spot, head : head + 1, :])
-            inner = column_sum(joint[head * HD : (head + 1) * HD, :])
-            slopes = dot_nt(r.values[...], given_heads[head]) - inner
-            slopes = (probs * slopes).astype(BF)
-            r.active[:, lanes] = probs.astype(BF)
-            r.grad_hidden[:, lanes] = slopes
-            made.append(dot_nn(r.turned[head * HD : (head + 1) * HD, :], slopes))
-        r.grad_values[...] += dot_nn(r.active[...], jnp.concatenate(given_heads, axis=0))
-        r.grad_keys[...] += dot_nn(r.grad_hidden[...], jnp.concatenate(asked_heads, axis=0))
-        turned = jnp.transpose(jnp.concatenate(made, axis=0)) * 0.125
-        r.grad_proj[rows, :heads_width] = turned.astype(BF)
+
+        def unmix(start, size):
+            near = rows_at(start, size)
+            mask_of(rows, near, size)
+            made = []
+            for head in range(heads):
+                lanes = slice(head * BLOCK, (head + 1) * BLOCK)
+                scores = dot_nt(r.keys[near, :], asked_heads[head]) + r.mask[0:size, :]
+                probs = jnp.exp(scores - r.stats[spot, head : head + 1, :])
+                inner = column_sum(joint[head * HD : (head + 1) * HD, :])
+                slopes = dot_nt(r.values[near, :], given_heads[head]) - inner
+                slopes = (probs * slopes).astype(BF)
+                r.active[0:size, lanes] = probs.astype(BF)
+                r.grad_hidden[0:size, lanes] = slopes
+                made.append(dot_nn(r.turned[head * HD : (head + 1) * HD, near], slopes))
+            given_tall = jnp.concatenate(given_heads, axis=0)
+            asked_tall = jnp.concatenate(asked_heads, axis=0)
+            r.grad_values[near, :] += dot_nn(r.active[0:size, :], given_tall)
+            r.grad_keys[near, :] += dot_nn(r.grad_hidden[0:size, :], asked_tall)
+            turned = jnp.transpose(jnp.concatenate(made, axis=0)) * 0.125
+            r.grad_proj[rows, :heads_width] = turned.astype(BF)
+
+        by_span(spot, unmix)
 
     links.sent(sum_one.side_in + sum_one.home_in)
     sum_four = RowSum(links, r.part_one, r.side_one, r.home_one, r.far_one)
@@ -758,6 +789,17 @@
         made = dot_nt(r.grad_proj[rows, :], flat_weight(r.full_a, r.wide, 0, qkv))
         r.part_one[rows, :] = made.astype(BF)
 
+    scatter_o = GradScatter(
+        links, r.grads_a, r.beside_a, r.landed_a, r.out_a, width * 5 // 6, width
+    )
+
+    @pl.loop(0, width // block)
+    def weigh_out(at):
+        columns = rows_at(at * block, block)
+        split_rows(dot_tn(r.rows_all[:, columns], r.mixed[...]), r.grads_a, at * block, r.wide, qkv)
+
+    scatter_o.begin()
+
     @pl.loop(0, 2)
     def project_remote(at):
         rows = rows_at((me ^ (3 - at)) * block, block)
@@ -780,7 +822,7 @@
     middle_lane = width // 2
     scatter_a = [
         GradScatter(links, r.grads_a, r.beside_a, r.landed_a, r.out_a, *lanes)
-        for lanes in ((0, middle_lane), (middle_lane, width))
+        for lanes in ((0, middle_lane), (middle_lane, width * 5 // 6))
     ]
 
     @pl.loop(0, width // block)
@@ -790,17 +832,13 @@
         split_rows(made, r.grads_a, at * block, r.wide, 0)
 
     scatter_a[0].begin()
+    for step in range(1, links.num_far):
+        scatter_o.pass_on(step)
 
     @pl.loop(0, width // block)
     def weigh_in_too(at):
         columns = rows_at(at * block, block)
-        made = jnp.concatenate(
-            [
-                dot_tn(r.normed[:, columns], r.grad_proj[:, middle_lane:qkv]),
-                dot_tn(r.rows_all[:, columns], r.mixed[...]),
-            ],
-            axis=1,
-        )
+        made = dot_tn(r.normed[:, columns], r.grad_proj[:, middle_lane:qkv])
         split_rows(made, r.grads_a, at * block, r.wide, middle_lane)
 
     scatter_a[1].begin()
@@ -815,10 +853,22 @@
         grad = sum_four.total(chunk)
         back, unit = layer_norm_back(r.frames[cut, :].astype(F32), grad, vec(gain_one))
         r.grad_frames[cut, :] = r.grad_middle[cut, :] + back
+        keep_result("grad_frames", cut)
         r.small_grads[gain_one : gain_one + 1, :] += column_sum(grad * unit)
         r.small_grads[shift_one : shift_one + 1, :] += column_sum(grad)
 
+    kept = []
+
+    def keep_result(name, cut=None):
+        source, place = getattr(r, name), getattr(r, name + "_hbm")
+        if cut is not None:
+            source, place = source.at[cut], place.at[cut]
+        made = pltpu.make_async_copy(source, place, r.local_sems.at[len(kept)])
+        made.start()
+        kept.append(made)
+
     scatter_b.end()
+    keep_result("out_b")
     scatter_a[0].pass_on(1)
     first_norm_back(0)
     for step in range(2, links.num_far):
@@ -827,6 +877,7 @@
         cut = sum_three.cut(chunk)
         row = r.middle[cut, :] + (sum_three.total(chunk) + vec(bias_fc2))
         r.output[cut, :] = row.astype(BF)
+    keep_result("output")
     first_norm_back(1)
     scatter_a[1].pass_on(1)
     scatter_a[1].pass_on(2)
@@ -854,8 +905,11 @@
     for made in back_dp:
         made.start()
     scatter_c.end()
+    keep_result("out_c")
+    scatter_o.end()
     for scatter in scatter_a:
         scatter.end()
+    keep_result("out_a")
     for at, made in enumerate(back_dp):
         made.wait_recv()
         total = total + r.small_dp[at]
@@ -863,7 +917,10 @@
     r.small_out[0:6, :] = pltpu.roll(total[0:6, :], lax.rem(width - start, width), 1)
     start = dp * share
     r.small_out[6:8, :] = pltpu.roll(total[6:8, :], lax.rem(width - start, width), 1)
+    keep_result("small_out")
     links.finish()
+    for made in kept:
+        made.wait()
 
 
 def copy_count(num_dp):
@@ -872,7 +929,7 @@
     spreads = 4 * 3 * CHUNKS
     weights = (3 + 2 + 2) * (2 * far - 1)
     sums = 4 * 3 * CHUNKS
-    scatters = 4 * (2 * far - 1)
+    scatters = 5 * (2 * far - 1)
     return smalls + spreads + weights + sums + scatters
 
 
@@ -943,15 +1000,19 @@
     for name in ("small_group", "small_group_back"):
         scratch += [(name, (3, 8, width), F32)]
     scratch += [("small_dp", (num_dp - 1, 8, width), F32)]
+    scratch += outputs
+    outputs = [(name + "_hbm", shape, kind) for name, shape, kind in outputs]
     count = copy_count(num_dp)
-    names = [name for name, _, _ in inputs + outputs + scratch] + ["send_sems", "recv_sems"]
+    names = [name for name, _, _ in inputs + outputs + scratch]
+    names += ["send_sems", "recv_sems", "local_sems"]
     return pl.pallas_call(
         functools.partial(layer_kernel, num_dp, names),
         out_shape=[jax.ShapeDtypeStruct(shape, kind) for _, shape, kind in outputs],
         in_specs=[spec for _, _, spec in inputs],
-        out_specs=[vmem] * len(outputs),
+        out_specs=[pl.BlockSpec(memory_space=pl.ANY)] * len(outputs),
         scratch_shapes=[pltpu.VMEM(shape, kind) for _, shape, kind in scratch]
-        + [pltpu.SemaphoreType.DMA((count,))] * 2,
+        + [pltpu.SemaphoreType.DMA((count,))] * 2
+        + [pltpu.SemaphoreType.DMA((8,))],
         compiler_params=pltpu.CompilerParams(
             collective_id=0, has_side_effects=True, vmem_limit_bytes=VMEM_BYTES
         ),
@@ -959,16 +1020,29 @@
     )(*[value for _, value, _ in inputs])
 
 
-def unpack_kernel(own, share, output, grad_frames, grads_a, grads_b, grads_c, sums, output_too, grad_frames_too, g_in, g_proj, g_out, grads_b_too, g_fc1b, grads_c_too, vec_0, vec_1, vec_2, vec_3, vec_4, vec_5, sems):
-    pairs = (
-        (output, output_too),
-        (grad_frames, grad_frames_too),
-        (grads_b, grads_b_too),
-        (grads_c, grads_c_too),
-    )
-    copies = [pltpu.make_async_copy(*pair, sems.at[at]) for at, pair in enumerate(pairs)]
-    for made in copies:
+def unpack_kernel(own, share, output, grad_frames, grads_a_in, grads_b, grads_c, sums_in, output_too, grad_frames_too, g_in, g_proj, g_out, grads_b_too, g_fc1b, grads_c_too, vec_0, vec_1, vec_2, vec_3, vec_4, vec_5, output_v, grad_frames_v, grads_a, grads_b_v, grads_c_v, sums, in_sems, out_sems):
+    pieces = grad_frames.shape[0] // CHUNKS
+    cuts = [pl.ds(at * pieces, pieces) for at in range(CHUNKS)]
+    moves = [(sums_in, sums, None), (grads_a_in, grads_a, None)]
+    moves += [(grads_b, grads_b_v, grads_b_too), (grads_c, grads_c_v, grads_c_too)]
+    moves += [(output, output_v, output_too)]
+    moves += [
+        (grad_frames.at[cut], grad_frames_v.at[cut], grad_frames_too.at[cut]) for cut in cuts
+    ]
+    inward = [
+        pltpu.make_async_copy(source, held, in_sems.at[at])
+        for at, (source, held, _) in enumerate(moves)
+    ]
+    for made in inward:
         made.start()
+    inward[0].wait()
+    inward[1].wait()
+    copies = []
+    for at in range(2, len(moves)):
+        inward[at].wait()
+        made = pltpu.make_async_copy(moves[at][1], moves[at][2], out_sems.at[at])
+        made.start()
+        copies.append(made)
     heads_width = g_in.shape[2]
     for at in range(3):
         g_in[at] = grads_a[:, at * heads_width : (at + 1) * heads_width]
@@ -1008,9 +1082,10 @@
     return pl.pallas_call(
         functools.partial(unpack_kernel, own, share),
         out_shape=[jax.ShapeDtypeStruct(shape, kind) for shape, kind, _ in shapes],
-        in_specs=[vmem] * 6,
+        in_specs=[hbm] * 6,
         out_specs=[spec for _, _, spec in shapes],
-        scratch_shapes=[pltpu.SemaphoreType.DMA((4,))],
+        scratch_shapes=[pltpu.VMEM(value.shape, value.dtype) for value in results]
+        + [pltpu.SemaphoreType.DMA((2 + 3 + CHUNKS,))] * 2,
         compiler_params=pltpu.CompilerParams(vmem_limit_bytes=VMEM_BYTES),
         name="unpack",
     )(*results)

time: 151 us -> 149 us (0.987)
  Pallas kernels: 150 us -> 148 us
    pallas_call x1, Pallas kernels: 146 us -> 144 us  [layer(): pl.pallas_call(functools.partial(layer_kernel, num_dp, names), out_shape=...]
where the time goes in v5:
time: 149 us
  Pallas kernels  148 us (99%)
    pallas_call x1, Pallas kernels, layer(): pl.pallas_call(functools.partial(layer_kernel, num_dp, names), out_shape=...  144 us
    pallas_call x1, Pallas kernels, unpack(): pl.pallas_call(functools.partial(unpack_kernel, own, share), out_shape=[j...  3.46 us

profile of v5, /device:TPU:0, one launch (start us, length us, event | category | flops | bytes accessed | tf_op | source)
XLA Modules:
  0.0 148.5 jit_solution(16105798943070090982)
XLA Ops:
  0.7 144.2 %layer.1 = (bf16[384,768]{1,0:T(8,128)(2,1)}, f32[384,768]{1,0:T(8,128)}, f32[96,768]{1,0:T(8,128)}, f32[96,768]{1,0:T(8,128)}, f32[96,768]{1,0:T(8,128)}, /*index=5*/f32[8,768]{1,0:T(8,128)}) custom-call(s32[1,1536]{1,0:T(1,128)} %refs_0_.1, bf16[384,768]{1,0:T(8,128)(2,1)} %refs_1_.1, bf16[384,768]{1,0:T(8,128)(2,1)} %refs_2_.1, ...), custom_call_target="tpu_custom_call" | custom-call | tf_op jit(solution)/shard_map/layer/pallas_call | solution.py:1008
  144.9 3.5 %unpack.1 = (bf16[384,768]{1,0:T(8,128)(2,1)}, f32[384,768]{1,0:T(8,128)}, f32[3,96,192]{2,1,0:T(8,128)}, f32[3,2,8]{2,1,0:T(2,128)}, f32[192,96]{1,0:T(8,128)},...) custom-call(bf16[384,768]{1,0:T(8,128)(2,1)} %get-tuple-element.34.o, ...), custom_call_target="tpu_custom_call" | custom-call | tf_op jit(solution)/shard_map/unpack/pallas_call | solution.py:1082

commit v6 on v5

--- a/solution.py
+++ b/solution.py
@@ -355,7 +355,7 @@
     given_rows = RowSpread(links, r.cotangent, r.given_all)
     spread_a = WeightSpread(links, r.shard_a, r.full_a, (0, width // 2, width * 5 // 6, width))
     spread_b = WeightSpread(links, r.shard_b, r.full_b, (0, width // 2, width))
-    spread_c = WeightSpread(links, r.shard_c, r.full_c, (0, width // 2, width))
+    spread_c = WeightSpread(links, r.shard_c, r.full_c, (0, width // 2, width * 5 // 6, width))
 
     r.shard_a[:, :qkv] = jnp.concatenate([r.in_weight[at] for at in range(3)], axis=1)
     r.shard_a[:, qkv:] = turn(r.out_weight[...])
@@ -407,8 +407,8 @@
         spread_a.begin_beside(half)
     for chunk in range(CHUNKS):
         given_rows.give(chunk)
-    for spread in (spread_b, spread_c):
-        for half in range(2):
+    for spread, halves in ((spread_b, 2), (spread_c, 3)):
+        for half in range(halves):
             spread.begin(half)
             spread.begin_beside(half)
     for spread in (spread_a, spread_b, spread_c):
@@ -596,8 +596,8 @@
                 r.middle[cut, :] = row
                 r.normed_own[cut, :] = layer_norm(row, vec(gain_two), vec(shift_two)).astype(BF)
                 spread_two.give(chunk)
-                if chunk == 0:
-                    spread_c.forward(1)
+                if chunk < 2:
+                    spread_c.forward(1 + chunk)
                 spread_two.sibling_in[chunk].wait_recv()
 
         hide(pair_rows(at, me))
@@ -605,7 +605,7 @@
     links.sent(sum_one.far_in + frame_rows.corner_in)
     given_rows.await_sibling()
     given_rows.await_corner()
-    spread_c.end((0, 1))
+    spread_c.end((0, 1, 2))
 
     sum_two = RowSum(links, r.part_two, r.side_two, r.home_two, r.far_two)
     sum_three = RowSum(links, r.normed_two, r.side_three, r.home_three, r.far_three)
@@ -927,7 +927,7 @@
     far = num_dp // 2
     smalls = 2 * (num_dp - 1 + 3)
     spreads = 4 * 3 * CHUNKS
-    weights = (3 + 2 + 2) * (2 * far - 1)
+    weights = (3 + 2 + 3) * (2 * far - 1)
     sums = 4 * 3 * CHUNKS
     scatters = 5 * (2 * far - 1)
     return smalls + spreads + weights + sums + scatters

time: 149 us -> 149 us (level)
  no operation moved by 1% of the time
where the time goes in v6:
time: 149 us
  Pallas kernels  148 us (99%)
    pallas_call x1, Pallas kernels, layer(): pl.pallas_call(functools.partial(layer_kernel, num_dp, names), out_shape=...  144 us
    pallas_call x1, Pallas kernels, unpack(): pl.pallas_call(functools.partial(unpack_kernel, own, share), out_shape=[j...  3.46 us

profile of v6, /device:TPU:0, one launch (start us, length us, event | category | flops | bytes accessed | tf_op | source)
XLA Modules:
  0.0 148.7 jit_solution(15131518817232108576)
XLA Ops:
  0.7 144.4 %layer.1 = (bf16[384,768]{1,0:T(8,128)(2,1)}, f32[384,768]{1,0:T(8,128)}, f32[96,768]{1,0:T(8,128)}, f32[96,768]{1,0:T(8,128)}, f32[96,768]{1,0:T(8,128)}, /*index=5*/f32[8,768]{1,0:T(8,128)}) custom-call(s32[1,1536]{1,0:T(1,128)} %refs_0_.1, bf16[384,768]{1,0:T(8,128)(2,1)} %refs_1_.1, bf16[384,768]{1,0:T(8,128)(2,1)} %refs_2_.1, ...), custom_call_target="tpu_custom_call" | custom-call | tf_op jit(solution)/shard_map/layer/pallas_call | solution.py:1008
  145.0 3.5 %unpack.1 = (bf16[384,768]{1,0:T(8,128)(2,1)}, f32[384,768]{1,0:T(8,128)}, f32[3,96,192]{2,1,0:T(8,128)}, f32[3,2,8]{2,1,0:T(2,128)}, f32[192,96]{1,0:T(8,128)},...) custom-call(bf16[384,768]{1,0:T(8,128)(2,1)} %get-tuple-element.34.o, ...), custom_call_target="tpu_custom_call" | custom-call | tf_op jit(solution)/shard_map/unpack/pallas_call | solution.py:1082
